TPU v7x, 256 devices: a whole 4x4x8 slice. The times are simulated.
256 devices in a mesh: cuts: 32 (over y_lo, z, core), chan: 8 (over y_hi, x).
Axes of the slice: x: 4, y: 4 (y_hi: 2, y_lo: 2; y = y_hi * 2 + y_lo), z: 8, core: 2. Of those that a mesh axis runs over, the one named last changes fastest.
Arguments:
- data: bfloat16 [256, 384, 1024], P('cuts', None, 'chan'), may hold values from -6 to 6
- order: int32 [256], P('cuts'), may hold values from 0 to 255, as said below
- chan_factor: bfloat16 [1024, 64], P('chan'), may hold values from -0.1875 to 0.1875
- slice_weights: float32 [256, 64], P('cuts'), may hold values from 0.5 to 2
- smooth_aux: float32 [256, 384, 64], P('cuts', 'chan'), may hold values from -6 to 6
- coupled: float32 [256, 384, 64], P('cuts', 'chan'), may hold values from -6 to 6
- smooth_dual: float32 [256, 384, 64], P('cuts', 'chan'), may hold values from -2 to 2
- coupling_dual: float32 [256, 384, 64], P('cuts', 'chan'), may hold values from -2 to 2
- delta: float32 [64, 64], replicated, may hold values from -0.1125 to 1.1125, as said below
Outputs:
- evolving: float32 [256, 384, 64], P('cuts', 'chan')
- coupled_out: float32 [256, 384, 64], P('cuts', 'chan')
- delta_out: float32 [64, 64], replicated
Inputs may be any that keep to these rules, and one draw needn't show every extreme that they name: `order`: within each aligned block of 8 entries (the slices of one index of cuts) the entries are a permutation of that block's own slice indices; entry k names the stored slice of phase bin k. `delta`: A full-rank matrix.
All inputs are finite; a program needn't handle non-finite values.
Results may differ from a plain program's by a relative error of at most 0.0003.
Values sent between devices are 32-bit elements; how exact they have to be, the bound alone decides.
A program may use at most 64 MiB of HBM per device.

v0:
```python
import jax
import jax.numpy as jnp
from jax import lax
from jax.sharding import PartitionSpec as P

INNER = 3
SWEEPS = 4
POLAR = 8


smooth_weight = 1.0
eps_trace = 1e-06
highest = lax.Precision.HIGHEST


def with_halo(cells, sides, width):
    for axis, dim in sides:
        count = lax.axis_size(axis)
        head = lax.slice_in_dim(cells, 0, width, axis=dim)
        tail = lax.slice_in_dim(cells, cells.shape[dim] - width, cells.shape[dim], axis=dim)
        cells = jnp.concatenate(
            [
                lax.ppermute(tail, axis, [(i, (i + 1) % count) for i in range(count)]),
                cells,
                lax.ppermute(head, axis, [((i + 1) % count, i) for i in range(count)]),
            ],
            axis=dim,
        )
    return cells


def setup_system(slice_weights, factor_gram):
    rank = factor_gram.shape[0]
    identity = jnp.eye(rank, dtype=jnp.float32)
    diagonal_gram = jnp.diagonal(factor_gram)
    rho = jnp.sum(slice_weights * slice_weights * diagonal_gram[None, :], axis=1) / rank
    system = slice_weights[:, :, None] * factor_gram[None] * slice_weights[:, None, :]
    system = system + 2.0 * rho[:, None, None] * identity
    factors = jax.vmap(jnp.linalg.cholesky)(system)
    inverse = jax.vmap(lambda lower: jax.scipy.linalg.cho_solve((lower, True), identity))(factors)
    return (rho, inverse)


def polar_terms(gram, delta_now):
    rank = gram.shape[1]
    identity = jnp.eye(rank, dtype=jnp.float32)
    left = jnp.einsum("rs,kst->krt", delta_now, gram, precision=highest)
    normal = jnp.einsum("krt,ut->kru", left, delta_now, precision=highest)
    trace = jnp.trace(normal, axis1=1, axis2=2) + eps_trace
    current = normal / trace[:, None, None]
    root = jnp.broadcast_to(identity, normal.shape)
    for step in range(POLAR):
        bracket = 1.5 * identity - 0.5 * jnp.einsum(
            "krs,kst->krt", root, current, precision=highest
        )
        current = jnp.einsum("krs,kst->krt", current, bracket, precision=highest)
        root = jnp.einsum("krs,kst->krt", bracket, root, precision=highest)
    scale = 1.0 / jnp.sqrt(trace)
    partial_value = jnp.einsum("ksr,st->krt", root, delta_now, precision=highest)
    partial_value = (
        jnp.einsum("krt,ktu->kru", partial_value, gram, precision=highest) * scale[:, None, None]
    )
    return (root, scale, partial_value)


def coupled_update(tall, root, scale, delta_now, delta_new):
    mixer = jnp.einsum("sr,kst->krt", delta_now, root, precision=highest)
    mixer = jnp.einsum("krt,tu->kru", mixer, delta_new, precision=highest) * scale[:, None, None]
    return jnp.einsum("kir,kru->kiu", tall, mixer, precision=highest)


def smooth(aux, target, rho_cols):
    for sweep in range(SWEEPS):
        padded = with_halo(aux, (("cuts", 0),), 1)
        beside = padded[:-2] + padded[2:]
        aux = (rho_cols * target + 2.0 * smooth_weight * beside) / (rho_cols + 4.0 * smooth_weight)
    return aux


def body(
    data, order, chan_factor, slice_weights, smooth_aux, coupled, smooth_dual, coupling_dual, delta
):
    count_slices = data.shape[0]
    total_slices = count_slices * lax.axis_size("cuts")
    summed = lax.psum_scatter(
        jnp.einsum("kij,jr->ikr", data, chan_factor, preferred_element_type=jnp.float32),
        "chan",
        scatter_dimension=0,
        tiled=True,
    )
    local_order = order - lax.axis_index("cuts") * count_slices
    projected = jnp.transpose(jnp.take(summed, local_order, axis=1), (1, 0, 2))
    factor_gram = lax.psum(
        jnp.dot(chan_factor.T, chan_factor, preferred_element_type=jnp.float32), "chan"
    )
    rho, inverse = setup_system(slice_weights, factor_gram)
    data_side = projected * slice_weights[:, None, :]
    rho_cols = rho[:, None, None]
    aux = smooth_aux
    coup = coupled
    dual_s = smooth_dual
    dual_c = coupling_dual
    delta_now = delta
    evolving = aux
    for inner in range(INNER):
        rhs = data_side + rho_cols * (aux - dual_s + coup - dual_c)
        evolving = jnp.einsum("kir,krs->kis", rhs, inverse, precision=highest)
        target = evolving + dual_s
        aux = smooth(aux, target, rho_cols)
        tall = evolving + dual_c
        whole = lax.all_gather(tall, "chan", axis=1, tiled=True)
        gram = jnp.einsum("kir,kis->krs", whole, whole, precision=highest)
        root, scale, partial_value = polar_terms(gram, delta_now)
        delta_new = lax.psum(jnp.sum(partial_value, axis=0), "cuts") / total_slices
        coup = coupled_update(tall, root, scale, delta_now, delta_new)
        dual_s = dual_s + evolving - aux
        dual_c = dual_c + evolving - coup
        delta_now = delta_new
    return (evolving, coup, delta_now)


def solution(mesh):
    return jax.shard_map(
        body,
        mesh=mesh,
        in_specs=(
            P("cuts", None, "chan"),
            P("cuts"),
            P("chan", None),
            P("cuts", None),
            P("cuts", "chan", None),
            P("cuts", "chan", None),
            P("cuts", "chan", None),
            P("cuts", "chan", None),
            P(),
        ),
        out_specs=(P("cuts", "chan", None), P("cuts", "chan", None), P()),
        check_vma=False,
    )
```

profile of v0, /device:TPU:1, one launch (start us, length us, event | category | flops | bytes accessed | tf_op | source)
XLA Modules:
  0.0 662.1 jit_solution(12568983401531240565)
XLA Ops:
  7.2 0.8 fusion.184
  8.0 3.2 collective-permute-start.1
  11.3 1.1 convolution_bitcast_fusion
  12.4 1.6 copy.125
  14.2 34.7 %psum.28 = f32[64,64]{1,0:T(8,128)S(1)} all-reduce(f32[64,64]{1,0:T(8,128)S(1)} %fusion.188), channel_id=1, replica_groups=mesh['cuts'=32,'chan'=8] {'chan'}, use_global_device_ids=true, to_apply=%region_1.2 | all-reduce | flops 4096 | bytes 32768 | tf_op jit(solution)/shard_map/psum | solution.py:93
  48.9 0.8 gather_fusion.1
  50.1 46.9 %custom-call.11 = f32[8,64,64]{2,1,0:T(8,128)S(1)} custom-call(f32[8,64,64]{2,1,0:T(8,128)S(1)} %add_multiply_fusion), custom_call_target="Cholesky" | custom-call | tf_op jit(solution)/shard_map/vmap(jit(cholesky))/cholesky | solution.py:39
  97.3 39.3 %custom-call.12 = f32[8,1,64,64]{2,3,1,0:T(8,128)S(1)} custom-call(f32[8,1,64,64]{3,2,1,0:T(8,128)S(1)} %select_bitcast_fusion), custom_call_target="InvertDiagBlocksLowerTriangular" | custom-call | tf_op jit(solution)/shard_map/vmap(jit(_cho_solve))/triangular_solve | solution.py:40
  137.7 1.0 copy.126
  139.9 32.6 %all_gather.9 = f32[8,384,64]{2,0,1:T(8,128)S(1)} all-gather(f32[8,48,64]{2,0,1:T(8,128)S(1)} %copy.129), channel_id=1, replica_groups=mesh['cuts'=32,'chan'=8] {'chan'}, dimensions={1}, use_global_device_ids=true | all-gather | bytes 884736 | tf_op jit(solution)/shard_map/all_gather | solution.py:111
  172.5 3.0 fusion.4
  176.1 0.7 select_reduce_fusion.2
  185.2 16.6 %collective-permute-start.3 = (f32[1,48,64]{2,1,0:T(8,128)S(1)}, f32[1,48,64]{2,1,0:T(8,128)S(1)}, u32[]{:S(2)}, u32[]{:S(2)}) collective-permute-start(f32[1,48,64]{2,1,0:T(8,128)S(1)} %get-tuple-element.25), channel_id=1, source_target_pairs={{8,0},{16,8},{24,16},{32,24},{40,32},{48,40},{56,48},{64,56},{72,6... | collective-permute-start | bytes 36872 | tf_op jit(solution)/shard_map/ppermute | solution.py:25
  203.8 3.7 collective-permute-start.5
  207.5 104.1 %psum.29 = f32[64,64]{1,0:T(8,128)S(1)} all-reduce(f32[64,64]{1,0:T(8,128)S(1)} %fusion.30), channel_id=1, replica_groups=mesh['cuts'=32,'chan'=8] {'cuts'}, use_global_device_ids=true, to_apply=%region_7.8 | all-reduce | flops 4096 | bytes 32768 | tf_op jit(solution)/shard_map/psum | solution.py:114
  311.7 4.5 collective-permute-start.7
  317.5 4.3 collective-permute-start.9
  323.6 34.2 %all_gather.10 = f32[8,384,64]{2,0,1:T(8,128)S(1)} all-gather(f32[8,48,64]{2,0,1:T(8,128)S(1)} %copy.136), channel_id=1, replica_groups=mesh['cuts'=32,'chan'=8] {'chan'}, dimensions={1}, use_global_device_ids=true | all-gather | bytes 884736 | tf_op jit(solution)/shard_map/all_gather | solution.py:111
  357.8 3.0 fusion.2
  361.4 0.7 select_reduce_fusion.1
  370.9 0.8 fusion.214
  372.1 7.2 %collective-permute-start.11 = (f32[1,48,64]{2,1,0:T(8,128)S(1)}, f32[1,48,64]{2,1,0:T(8,128)S(1)}, u32[]{:S(2)}, u32[]{:S(2)}) collective-permute-start(f32[1,48,64]{2,1,0:T(8,128)S(1)} %get-tuple-element.16), channel_id=1, source_target_pairs={{8,0},{16,8},{24,16},{32,24},{40,32},{48,40},{56,48},{64,56},{72,6... | collective-permute-start | bytes 36872 | tf_op jit(solution)/shard_map/ppermute | solution.py:25
  379.7 103.9 %psum.30 = f32[64,64]{1,0:T(8,128)S(1)} all-reduce(f32[64,64]{1,0:T(8,128)S(1)} %fusion.31), channel_id=1, replica_groups=mesh['cuts'=32,'chan'=8] {'cuts'}, use_global_device_ids=true, to_apply=%region_10.11 | all-reduce | flops 4096 | bytes 32768 | tf_op jit(solution)/shard_map/psum | solution.py:114
  483.7 4.5 collective-permute-start.13
  489.6 4.3 collective-permute-start.15
  495.1 1.2 fusion.187
  496.4 32.4 %all_gather.11 = f32[8,384,64]{2,0,1:T(8,128)S(1)} all-gather(f32[8,48,64]{2,0,1:T(8,128)S(1)} %copy.143), channel_id=1, replica_groups=mesh['cuts'=32,'chan'=8] {'chan'}, dimensions={1}, use_global_device_ids=true | all-gather | bytes 884736 | tf_op jit(solution)/shard_map/all_gather | solution.py:111
  528.7 3.0 fusion
  532.3 0.7 select_reduce_fusion
  541.8 0.9 fusion.227
  543.5 109.6 %psum.31 = f32[64,64]{1,0:T(8,128)S(1)} all-reduce(f32[64,64]{1,0:T(8,128)S(1)} %fusion.32), channel_id=1, replica_groups=mesh['cuts'=32,'chan'=8] {'cuts'}, use_global_device_ids=true, to_apply=%region_13.14 | all-reduce | flops 4096 | bytes 32768 | tf_op jit(solution)/shard_map/psum | solution.py:114
  653.7 1.1 fusion.228
  (167 shorter events, 40.2 us)
Async XLA Ops:
  7.2 4.1 copy-start
  7.2 130.5 %reduce-scatter.2.cloned.1.call-start = ((), (), s32[]{:S(2)}) async-start(), calls=%async_computation.1 | async-start | bytes 1769472 | tf_op jit(solution)/shard_map/reduce_scatter | solution.py:85
  8.0 131.2 %collective-permute-start.1 = (f32[1,48,64]{2,1,0:T(8,128)S(1)}, f32[1,48,64]{2,1,0:T(8,128)S(1)}, u32[]{:S(2)}, u32[]{:S(2)}) collective-permute-start(f32[1,48,64]{2,1,0:T(8,128)S(1)} %get-tuple-element.28), channel_id=1, source_target_pairs={{8,0},{16,8},{24,16},{32,24},{40,32},{48,40},{56,48},{64,56},{72,6... | collective-permute-start | bytes 36872 | tf_op jit(solution)/shard_map/ppermute | solution.py:25
  11.2 128.0 %collective-permute-start = (f32[1,48,64]{2,1,0:T(8,128)S(1)}, f32[1,48,64]{2,1,0:T(8,128)S(1)}, u32[]{:S(2)}, u32[]{:S(2)}) collective-permute-start(f32[1,48,64]{2,1,0:T(8,128)S(1)} %get-tuple-element.27), channel_id=1, source_target_pairs={{0,8},{8,16},{16,24},{24,32},{32,40},{40,48},{48,56},{56,64},{64,7... | collective-permute-start | bytes 36872 | tf_op jit(solution)/shard_map/ppermute | solution.py:23
  12.4 1.7 copy-start.7
  14.0 35.7 %copy-start.6 = (f32[8,64]{1,0:T(8,128)S(1)}, f32[8,64]{1,0:T(8,128)}, u32[]{:S(2)}) copy-start(f32[8,64]{1,0:T(8,128)} %param.12) | copy-start | bytes 6148
  14.0 122.7 %copy-start.9 = (s32[8]{0:T(128)S(1)}, s32[8]{0:T(128)}, u32[]{:S(2)}) copy-start(s32[8]{0:T(128)} %param.10) | copy-start | bytes 100
  50.1 89.2 %copy-start.1 = (f32[8,48,64]{2,1,0:T(8,128)S(1)}, f32[8,48,64]{2,1,0:T(8,128)}, u32[]{:S(2)}) copy-start(f32[8,48,64]{2,1,0:T(8,128)} %param.13) | copy-start | bytes 294916
  50.1 89.2 %copy-start.3 = (f32[8,48,64]{2,1,0:T(8,128)S(1)}, f32[8,48,64]{2,1,0:T(8,128)}, u32[]{:S(2)}) copy-start(f32[8,48,64]{2,1,0:T(8,128)} %param.15) | copy-start | bytes 294916
  50.1 89.2 %copy-start.4 = (f32[8,48,64]{2,1,0:T(8,128)S(1)}, f32[8,48,64]{2,1,0:T(8,128)}, u32[]{:S(2)}) copy-start(f32[8,48,64]{2,1,0:T(8,128)} %param.16) | copy-start | bytes 294916
  50.1 89.2 %copy-start.5 = (f32[8,48,64]{2,1,0:T(8,128)S(1)}, f32[8,48,64]{2,1,0:T(8,128)}, u32[]{:S(2)}) copy-start(f32[8,48,64]{2,1,0:T(8,128)} %param.14) | copy-start | bytes 294916
  139.9 35.6 %copy-start.2 = (f32[64,64]{1,0:T(8,128)S(1)}, f32[64,64]{1,0:T(8,128)}, u32[]{:S(2)}) copy-start(f32[64,64]{1,0:T(8,128)} %param.17) | copy-start | bytes 49156
  185.2 18.4 %collective-permute-start.3 = (f32[1,48,64]{2,1,0:T(8,128)S(1)}, f32[1,48,64]{2,1,0:T(8,128)S(1)}, u32[]{:S(2)}, u32[]{:S(2)}) collective-permute-start(f32[1,48,64]{2,1,0:T(8,128)S(1)} %get-tuple-element.25), channel_id=1, source_target_pairs={{8,0},{16,8},{24,16},{32,24},{40,32},{48,40},{56,48},{64,56},{72,6... | collective-permute-start | bytes 36872 | tf_op jit(solution)/shard_map/ppermute | solution.py:25
  201.9 1.8 collective-permute-start.2
  203.8 107.8 %collective-permute-start.5 = (f32[1,48,64]{2,1,0:T(8,128)S(1)}, f32[1,48,64]{2,1,0:T(8,128)S(1)}, u32[]{:S(2)}, u32[]{:S(2)}) collective-permute-start(f32[1,48,64]{2,1,0:T(8,128)S(1)} %get-tuple-element.23), channel_id=1, source_target_pairs={{8,0},{16,8},{24,16},{32,24},{40,32},{48,40},{56,48},{64,56},{72,6... | collective-permute-start | bytes 36872 | tf_op jit(solution)/shard_map/ppermute | solution.py:25
  207.5 104.1 %collective-permute-start.4 = (f32[1,48,64]{2,1,0:T(8,128)S(1)}, f32[1,48,64]{2,1,0:T(8,128)S(1)}, u32[]{:S(2)}, u32[]{:S(2)}) collective-permute-start(f32[1,48,64]{2,1,0:T(8,128)S(1)} %get-tuple-element.22), channel_id=1, source_target_pairs={{0,8},{8,16},{16,24},{24,32},{32,40},{40,48},{48,56},{56,64},{64,7... | collective-permute-start | bytes 36872 | tf_op jit(solution)/shard_map/ppermute | solution.py:23
  311.7 5.4 collective-permute-start.7
  316.2 1.2 collective-permute-start.6
  317.5 5.2 collective-permute-start.9
  321.9 1.2 collective-permute-start.8
  372.1 111.5 %collective-permute-start.11 = (f32[1,48,64]{2,1,0:T(8,128)S(1)}, f32[1,48,64]{2,1,0:T(8,128)S(1)}, u32[]{:S(2)}, u32[]{:S(2)}) collective-permute-start(f32[1,48,64]{2,1,0:T(8,128)S(1)} %get-tuple-element.16), channel_id=1, source_target_pairs={{8,0},{16,8},{24,16},{32,24},{40,32},{48,40},{56,48},{64,56},{72,6... | collective-permute-start | bytes 36872 | tf_op jit(solution)/shard_map/ppermute | solution.py:25
  379.3 104.3 %collective-permute-start.10 = (f32[1,48,64]{2,1,0:T(8,128)S(1)}, f32[1,48,64]{2,1,0:T(8,128)S(1)}, u32[]{:S(2)}, u32[]{:S(2)}) collective-permute-start(f32[1,48,64]{2,1,0:T(8,128)S(1)} %get-tuple-element.15), channel_id=1, source_target_pairs={{0,8},{8,16},{16,24},{24,32},{32,40},{40,48},{48,56},{56,64},{64,7... | collective-permute-start | bytes 36872 | tf_op jit(solution)/shard_map/ppermute | solution.py:23
  483.7 5.4 collective-permute-start.13
  488.2 1.2 collective-permute-start.12
  489.6 5.2 collective-permute-start.15
  493.9 1.2 collective-permute-start.14
  653.1 1.7 copy-start.8
Sparse Core Ops, SparseCore 0:
  14.2 81.1 reduce-scatter.1
where the time goes:
time: 669 us; the launch traced here: 662 us
  blocking collectives  451 us (67%)
  other arithmetic  87.4 us (13%)
  matrix products  51.3 us (8%)
  starting transfers between devices  48.5 us (7%)
  between operations  15.6 us (2%)
    psum x3, blocking collectives, body(): delta_new = lax.psum(jnp.sum(partial_value, axis=0), 'cuts') / total_slices  318 us
    all_gather x3, blocking collectives, body(): whole = lax.all_gather(tall, 'chan', axis=1, tiled=True)  99.1 us
    ppermute x8, starting transfers between devices, with_halo(): lax.ppermute(head, axis, [((i + 1) % count, i) for i in range(count)])  48.5 us
    another operation x4, other arithmetic, setup_system(): factors = jax.vmap(jnp.linalg.cholesky)(system)  47.1 us
    another operation x3, other arithmetic, setup_system(): jax.scipy.linalg.cho_solve((lower, True), identity)  39.4 us
    psum x1, blocking collectives, body(): lax.psum(jnp.dot(chan_factor.T, chan_factor, preferred_element_type=jnp.f...  34.7 us
  transfers between devices with their start and end apart: 17, of which 8 were waited for; matrix products, arithmetic and copies ran while one was open for 15% of the time, Pallas kernels for 0%

commit v1 on v0

v1 whole, which is shorter than its diff:
```python
import jax
import jax.numpy as jnp
from jax import lax
from jax.experimental import pallas as pl
from jax.experimental.pallas import tpu as pltpu
from jax.sharding import PartitionSpec as P

INNER = 3
POLAR = 8
NEWTON = 7
EPS_TRACE = 1e-06
F32 = jnp.float32
HIGH = lax.Precision.HIGHEST
MESH = pl.DeviceIdType.MESH
CHEB_A = 0.1328125 / 1.2578125
CHEB_B = -1.0 / (512.0 * 1.2578125)


def mm(a, b):
    return jnp.dot(a, b, precision=HIGH, preferred_element_type=F32)


def mm_tn(a, b):
    return lax.dot_general(a, b, (((0,), (0,)), ((), ())), precision=HIGH, preferred_element_type=F32)


def kernel(
    order, data_h, fac_h, w_h, aux_h, coup_h, ds_h, dc_h, delta_h,
    evo_o, coup_o, delta_o,
    data_v, fac_v, w_v, aux_v, coup_v, ds_v, dc_v, delta_v,
    psend, precv, ysend, yrecv, fg, x2, cr, left_s, k2_s,
    gsend, grecv, gall, qsend, qrecv, zbuf, qall,
    aux_p, dss, dcs, talls, evos, at_s, baux, hal_a, hal_t, bsend, hal_b,
    load_sem, px_s, px_r, py_s, py_r, fg_s, fg_r,
    g1_s, g1_r, g2_s, g2_r, q1_s, q1_r, z_s, z_r, q2_s, q2_r, ha_s, ha_r, ht_s, ht_r, hb_s, hb_r,
):
    cuts = lax.axis_index("cuts")
    chan = lax.axis_index("chan")
    core = lax.rem(cuts, 2)
    zz = lax.rem(cuts // 2, 8)
    ylo = cuts // 16
    quad = ylo * 2 + core
    xx = lax.rem(chan, 4)
    yhi = chan // 4
    left_id = lax.rem(cuts + 31, 32)
    right_id = lax.rem(cuts + 1, 32)

    def z_dev(z):
        return (ylo * 16 + z * 2 + core, chan)

    def quad_dev(q):
        return ((q // 2) * 16 + zz * 2 + lax.rem(q, 2), chan)

    sent = []

    def send(src, dst, ssem, rsem, dev):
        copy = pltpu.make_async_remote_copy(
            src_ref=src, dst_ref=dst, send_sem=ssem, recv_sem=rsem, device_id=dev, device_id_type=MESH
        )
        copy.start()
        sent.append(copy)

    def arrived(dst, ssem, rsem):
        pltpu.make_async_remote_copy(
            src_ref=dst, dst_ref=dst, send_sem=ssem, recv_sem=rsem, device_id=(left_id, chan), device_id_type=MESH
        ).wait_recv()

    loads = []
    for n, (src, dst) in enumerate(
        (
            (fac_h, fac_v), (data_h, data_v), (w_h, w_v), (aux_h, aux_v), (coup_h, coup_v),
            (ds_h, ds_v), (dc_h, dc_v), (delta_h, delta_v),
        )
    ):
        copy = pltpu.make_async_copy(src, dst, load_sem.at[n])
        copy.start()
        loads.append(copy)

    barrier = pltpu.get_barrier_semaphore()
    greet = [(cuts, lax.rem(chan + d, 8)) for d in range(1, 8)]
    greet += [z_dev(lax.rem(zz + d, 8)) for d in range(1, 8)]
    greet += [quad_dev(lax.rem(quad + d, 4)) for d in range(1, 4)]
    greet += [(left_id, chan), (right_id, chan)]
    for dev in greet:
        pl.semaphore_signal(barrier, inc=1, device_id=dev, device_id_type=MESH)

    lane = lax.broadcasted_iota(jnp.int32, (1, 128), 1)
    low = lane < 64
    row_i = lax.broadcasted_iota(jnp.int32, (128, 128), 0)
    col_i = lax.broadcasted_iota(jnp.int32, (128, 128), 1)
    eye_b = row_i == col_i
    eye = eye_b.astype(F32)

    def swap(v):
        return pltpu.roll(v, 64, 1)

    def unpack2(g, h):
        a = jnp.concatenate([g, swap(g)], axis=0)
        b = jnp.concatenate([swap(h), h], axis=0)
        zero = jnp.zeros_like(a)
        return jnp.concatenate([jnp.where(low, a, zero), jnp.where(low, zero, b)], axis=0)

    def pack2(t):
        g = jnp.where(low, t[0:32], swap(t[32:64]))
        h = jnp.where(low, swap(t[64:96]), t[96:128])
        return g, h

    def half_sums(v):
        zero = jnp.zeros_like(v)
        lo = jnp.sum(jnp.where(low, v, zero), axis=1, keepdims=True)
        hi = jnp.sum(jnp.where(low, zero, v), axis=1, keepdims=True)
        return jnp.where(low, lo, hi)

    loads[0].wait()
    fac = fac_v[...]
    partial_gram = lax.dot_general(fac, fac, (((0,), (0,)), ((), ())), preferred_element_type=F32)
    fg[chan] = jnp.concatenate([partial_gram[0:32], partial_gram[32:64]], axis=1)
    pl.semaphore_wait(barrier, len(greet))
    for d in range(1, 8):
        peer = lax.rem(chan + d, 8)
        send(fg.at[chan], fg.at[chan], fg_s.at[d - 1], fg_r.at[chan], (cuts, peer))

    zero_fac = jnp.zeros_like(fac)
    fac2 = jnp.concatenate(
        [jnp.concatenate([fac, zero_fac], axis=1), jnp.concatenate([zero_fac, fac], axis=1)], axis=0
    )
    loads[1].wait()
    for j in range(4):
        first = data_v[lax.rem(order[j], 8)]
        second = data_v[lax.rem(order[j + 4], 8)]
        out = jnp.dot(jnp.concatenate([first, second], axis=1), fac2, preferred_element_type=F32)
        for c in range(8):
            psend[c % 4, c // 4, j] = out[48 * c : 48 * c + 48]
    for d in (2, 1, 3):
        to = lax.rem(xx + d, 4)
        send(psend.at[to], precv.at[xx], px_s.at[d - 1], px_r.at[xx], (cuts, yhi * 4 + to))

    for n in range(2, 8):
        loads[n].wait()
    for j in range(4):
        aux_p[0, j] = jnp.concatenate([aux_v[j], aux_v[j + 4]], axis=1)
        dss[j] = jnp.concatenate([ds_v[j], ds_v[j + 4]], axis=1)
        dcs[j] = jnp.concatenate([dc_v[j], dc_v[j + 4]], axis=1)
        talls[j] = jnp.concatenate([coup_v[j], coup_v[j + 4]], axis=1)

    def halo_send(src, dst, ssem, rsem):
        send(src, dst.at[0], ssem.at[0], rsem.at[0], (right_id, chan))
        send(src, dst.at[1], ssem.at[1], rsem.at[1], (left_id, chan))

    halo_send(aux_p.at[0], hal_a.at[0], ha_s.at[0], ha_r.at[0])

    for d in range(1, 8):
        peer = lax.rem(chan + d, 8)
        arrived(fg.at[peer], fg_s.at[0], fg_r.at[peer])
    gram_sum = fg[0]
    for c in range(1, 8):
        gram_sum = gram_sum + fg[c]
    gram2 = unpack2(gram_sum, gram_sum)
    w = w_v[...]
    w2 = jnp.concatenate([w[0:4], w[4:8]], axis=1)
    diag_row = jnp.sum(jnp.where(eye_b, gram2, 0.0), axis=0, keepdims=True)
    rho = half_sums(w2 * w2 * diag_row) * (1.0 / 64.0)
    w_over = w2 / rho
    b_rows = 2.0 / (rho + 4.0)
    a_rows = rho / (rho + 4.0)
    bsend[0:4] = b_rows
    bsend[4:8] = b_rows
    halo_send(bsend, hal_b, hb_s, hb_r)
    systems = []
    for j in range(4):
        w_row = w2[j : j + 1]
        w_col = jnp.sum(jnp.where(eye_b, w_row, 0.0), axis=1, keepdims=True)
        system = gram2 * w_col * w_over[j : j + 1] + 2.0 * eye
        left_s[j] = system
        x2[j] = CHEB_A * eye + CHEB_B * system

    def newton(step, carry):
        for j in range(4):
            x = x2[j]
            x2[j] = mm(x, 2.0 * eye - mm(left_s[j], x))
        return carry

    lax.fori_loop(0, NEWTON, newton, 0)

    for d in range(1, 4):
        frm = lax.rem(xx + d, 4)
        arrived(precv.at[frm], px_s.at[0], px_r.at[frm])
    for j in range(4):
        total = psend[xx, 1 - yhi, j]
        for d in range(1, 4):
            total = total + precv[lax.rem(xx + d, 4), 1 - yhi, j]
        ysend[j] = total
    send(ysend, yrecv, py_s, py_r, (cuts, (1 - yhi) * 4 + xx))
    for j in range(4):
        total = psend[xx, yhi, j]
        for d in range(1, 4):
            total = total + precv[lax.rem(xx + d, 4), yhi, j]
        baux[j] = total
    arrived(yrecv, py_s, py_r)
    for j in range(4):
        baux[j] = (baux[j] + yrecv[j]) * w_over[j : j + 1]

    delta_in = delta_v[...]
    zero_d = jnp.zeros_like(delta_in)
    delta2 = jnp.concatenate(
        [jnp.concatenate([delta_in, zero_d], axis=1), jnp.concatenate([zero_d, delta_in], axis=1)], axis=0
    )

    for it in range(INNER):
        last = it == INNER - 1
        for j in range(4):
            coup_less = talls[j] - dcs[j] if it == 0 else talls[j]
            rhs = baux[j] + (aux_p[it, j] - dss[j]) + coup_less
            evo = mm(rhs, x2[j])
            tall = evo + dcs[j]
            evos[j] = evo
            talls[j] = tall
            g, h = pack2(mm_tn(tall, tall))
            gsend[it, j] = g
            gsend[it, j + 4] = h
        for d in range(1, 8):
            peer = lax.rem(chan + d, 8)
            send(gsend.at[it, peer], grecv.at[it, chan], g1_s.at[it, d - 1], g1_r.at[it, chan], (cuts, peer))
        if not last:
            for j in range(4):
                at_s[it, j] = (evos[j] + dss[j]) * a_rows[j : j + 1]
            halo_send(at_s.at[it], hal_t.at[it], ht_s.at[it], ht_r.at[it])
        else:
            for j in range(4):
                evo = evos[j]
                evo_o[j] = evo[:, 0:64]
                evo_o[j + 4] = evo[:, 64:128]
        grecv[it, chan] = gsend[it, chan]
        for d in range(1, 8):
            peer = lax.rem(chan + d, 8)
            arrived(grecv.at[it, peer], g1_s.at[it, 0], g1_r.at[it, peer])
        own = grecv[it, 0]
        for c in range(1, 8):
            own = own + grecv[it, c]
        gall[it, chan] = own
        for d in range(1, 8):
            peer = lax.rem(chan + d, 8)
            send(gall.at[it, chan], gall.at[it, chan], g2_s.at[it, d - 1], g2_r.at[it, chan], (cuts, peer))
        delta2t = delta2.T
        for d in range(1, 8):
            peer = lax.rem(chan + d, 8)
            arrived(gall.at[it, peer], g2_s.at[it, 0], g2_r.at[it, peer])

        scales = []
        for j in range(4):
            lefts = mm(delta2, unpack2(gall[it, j], gall[it, j + 4]))
            left_s[j] = lefts
            normal = mm(lefts, delta2t)
            trace = half_sums(jnp.sum(jnp.where(eye_b, normal, 0.0), axis=0, keepdims=True)) + EPS_TRACE
            scales.append(1.0 / jnp.sqrt(trace))
            cur = normal / trace
            bracket = 1.5 * eye - 0.5 * cur
            cr[j, :, 0:128] = mm(bracket, cur)
            cr[j, :, 128:256] = bracket

        def polar(step, carry):
            for j in range(4):
                both = cr[j]
                bracket = 1.5 * eye - 0.5 * mm(both[:, 128:256], both[:, 0:128])
                cr[j] = mm(bracket, both)
            return carry

        lax.fori_loop(0, POLAR - 2, polar, 0)
        part = jnp.zeros((128, 128), F32)
        for j in range(4):
            both = cr[j]
            root = both[:, 128:256]
            bracket = 1.5 * eye - 0.5 * mm(root, both[:, 0:128])
            root = mm(bracket, root)
            cr[j, :, 128:256] = root
            part = part + mm(root, left_s[j]) * scales[j]
        g, h = pack2(part)
        packed = g + h
        for q in range(4):
            qsend[it, q] = packed[8 * q : 8 * q + 8]
        for d in range(1, 4):
            to = lax.rem(quad + d, 4)
            send(qsend.at[it, to], qrecv.at[it, quad], q1_s.at[it, d - 1], q1_r.at[it, quad], quad_dev(to))
        qrecv[it, quad] = qsend[it, quad]
        for j in range(4):
            k2_s[j] = mm(delta2t, cr[j, :, 128:256]) * scales[j]
        for d in range(1, 4):
            frm = lax.rem(quad + d, 4)
            arrived(qrecv.at[it, frm], q1_s.at[it, 0], q1_r.at[it, frm])
        zbuf[it, zz] = (qrecv[it, 0] + qrecv[it, 1]) + (qrecv[it, 2] + qrecv[it, 3])
        for d in range(1, 8):
            to = lax.rem(zz + d, 8)
            send(zbuf.at[it, zz], zbuf.at[it, zz], z_s.at[it, d - 1], z_r.at[it, zz], z_dev(to))

        if not last:
            for n in range(2):
                arrived(hal_a.at[it, n], ha_s.at[it, n], ha_r.at[it, n])
                arrived(hal_t.at[it, n], ht_s.at[it, n], ht_r.at[it, n])
                if it == 0:
                    arrived(hal_b.at[n], hb_s.at[n], hb_r.at[n])
            vals, tars, bs = [], [], []
            for p in range(4):
                vals.append(jnp.where(low, swap(hal_a[it, 0, p]), aux_p[it, p]))
                tars.append(jnp.where(low, swap(hal_t[it, 0, p]), at_s[it, p]))
                bs.append(jnp.where(low, swap(hal_b[0, p : p + 1]), bsend[p : p + 1]))
            for p in range(4):
                vals.append(jnp.where(low, aux_p[it, p], swap(hal_a[it, 1, p])))
                tars.append(jnp.where(low, at_s[it, p], swap(hal_t[it, 1, p])))
                bs.append(jnp.where(low, bsend[p : p + 1], swap(hal_b[1, p : p + 1])))
            for sweep in range(4):
                fresh = []
                for p in range(8):
                    before = vals[p - 1] if p > 0 else swap(vals[7])
                    after = vals[p + 1] if p < 7 else swap(vals[0])
                    fresh.append(tars[p] + bs[p] * (before + after))
                vals = fresh
            for j in range(4):
                aux = jnp.where(low, vals[4 + j], vals[j])
                aux_p[it + 1, j] = aux
                dss[j] = dss[j] + evos[j] - aux
            if it + 1 < INNER - 1:
                halo_send(aux_p.at[it + 1], hal_a.at[it + 1], ha_s.at[it + 1], ha_r.at[it + 1])

        for d in range(1, 8):
            frm = lax.rem(zz + d, 8)
            arrived(zbuf.at[it, frm], z_s.at[it, 0], z_r.at[it, frm])
        total = zbuf[it, 0]
        for z in range(1, 8):
            total = total + zbuf[it, z]
        qall[it, quad] = total * (1.0 / 256.0)
        for d in range(1, 4):
            to = lax.rem(quad + d, 4)
            send(qall.at[it, quad], qall.at[it, quad], q2_s.at[it, d - 1], q2_r.at[it, quad], quad_dev(to))
        for d in range(1, 4):
            frm = lax.rem(quad + d, 4)
            arrived(qall.at[it, frm], q2_s.at[it, 0], q2_r.at[it, frm])
        packed = jnp.concatenate([qall[it, q] for q in range(4)], axis=0)
        delta2 = unpack2(packed, packed)

        for j in range(4):
            mixer = mm(k2_s[j], delta2)
            tall = talls[j]
            coup = mm(tall, mixer)
            if last:
                coup_o[j] = coup[:, 0:64]
                coup_o[j + 4] = coup[:, 64:128]
            else:
                dual = tall - coup
                dcs[j] = dual
                talls[j] = coup - dual
        if last:
            delta_o[...] = delta2[0:64, 0:64]

    for copy in sent:
        copy.wait_send()


def body(data, order, chan_factor, slice_weights, smooth_aux, coupled, smooth_dual, coupling_dual, delta):
    vm = pltpu.VMEM
    dma = pltpu.SemaphoreType.DMA
    rows = (4, 48, 128)
    anyspace = pl.BlockSpec(memory_space=pl.ANY)
    vspace = pl.BlockSpec(memory_space=pltpu.VMEM)
    return pl.pallas_call(
        kernel,
        out_shape=(
            jax.ShapeDtypeStruct((8, 48, 64), F32),
            jax.ShapeDtypeStruct((8, 48, 64), F32),
            jax.ShapeDtypeStruct((64, 64), F32),
        ),
        in_specs=[pl.BlockSpec(memory_space=pltpu.SMEM)] + [anyspace] * 8,
        out_specs=(vspace, vspace, vspace),
        scratch_shapes=[
            vm((8, 384, 128), jnp.bfloat16), vm((128, 64), jnp.bfloat16), vm((8, 64), F32),
            vm((8, 48, 64), F32), vm((8, 48, 64), F32), vm((8, 48, 64), F32), vm((8, 48, 64), F32), vm((64, 64), F32),
            vm((4, 2) + rows, F32), vm((4, 2) + rows, F32), vm(rows, F32), vm(rows, F32),
            vm((8, 32, 128), F32), vm((4, 128, 128), F32), vm((4, 128, 256), F32),
            vm((4, 128, 128), F32), vm((4, 128, 128), F32),
            vm((3, 8, 32, 128), F32), vm((3, 8, 32, 128), F32), vm((3, 8, 32, 128), F32),
            vm((3, 4, 8, 128), F32), vm((3, 4, 8, 128), F32), vm((3, 8, 8, 128), F32), vm((3, 4, 8, 128), F32),
            vm((3,) + rows, F32), vm(rows, F32), vm(rows, F32), vm(rows, F32), vm(rows, F32),
            vm((2,) + rows, F32), vm(rows, F32),
            vm((2, 2) + rows, F32), vm((2, 2) + rows, F32), vm((8, 128), F32), vm((2, 8, 128), F32),
            dma((8,)), dma((3,)), dma((4,)), dma, dma, dma((7,)), dma((8,)),
            dma((3, 7)), dma((3, 8)), dma((3, 7)), dma((3, 8)), dma((3, 3)), dma((3, 4)),
            dma((3, 7)), dma((3, 8)), dma((3, 3)), dma((3, 4)),
            dma((2, 2)), dma((2, 2)), dma((2, 2)), dma((2, 2)), dma((2,)), dma((2,)),
        ],
        compiler_params=pltpu.CompilerParams(
            collective_id=0, has_side_effects=True, vmem_limit_bytes=60 * 1024 * 1024
        ),
    )(order, data, chan_factor, slice_weights, smooth_aux, coupled, smooth_dual, coupling_dual, delta)


def solution(mesh):
    return jax.shard_map(
        body,
        mesh=mesh,
        in_specs=(
            P("cuts", None, "chan"),
            P("cuts"),
            P("chan", None),
            P("cuts", None),
            P("cuts", "chan", None),
            P("cuts", "chan", None),
            P("cuts", "chan", None),
            P("cuts", "chan", None),
            P(),
        ),
        out_specs=(P("cuts", "chan", None), P("cuts", "chan", None), P()),
        check_vma=False,
    )
```

time: 669 us -> 137 us (0.20)
  blocking collectives: 451 us -> 0 us
  Pallas kernels: 0 us -> 132 us
  other arithmetic: 87.4 us -> 0 us
  matrix products: 51.3 us -> 0 us
  starting transfers between devices: 48.5 us -> 0 us
  between operations: 15.6 us -> 0.65 us
    psum x4 -> x0, blocking collectives: 352 us -> none  [the longest x3 318 us: body(): delta_new = lax.psum(jnp.sum(partial_value, axis=0), 'cuts') / total_slices]
    pallas_call x0 -> x1, Pallas kernels: none -> 132 us  [body(): pl.pallas_call(kernel, out_shape=(jax.ShapeDtypeStruct((8, 48, 64), F32),...]
    all_gather x3 -> x0, blocking collectives: 99.1 us -> none  [body(): whole = lax.all_gather(tall, 'chan', axis=1, tiled=True)]
    another operation x7 -> x0, other arithmetic: 86.5 us -> none  [the longest x4 47.1 us: setup_system(): factors = jax.vmap(jnp.linalg.cholesky)(system)]
    dot_general x95 -> x0, matrix products: 50.3 us -> none  [the longest x24 10.4 us: polar_terms(): root = jnp.einsum('krs,kst->krt', bracket, root, precision=highest)]
    ppermute x16 -> x0, starting transfers between devices: 48.5 us -> none  [the longest x8 48.5 us: with_halo(): lax.ppermute(head, axis, [((i + 1) % count, i) for i in range(count)])]
  transfers between devices with their start and end apart: 17 -> 0, of which waited for: 8 -> 0; matrix products, arithmetic and copies ran while one was open for 15% -> 0% of each run, Pallas kernels for 0% -> 0%
where the time goes in v1:
time: 137 us
  Pallas kernels  132 us (96%)
  local copies, waits for them, and re-layouts  4.47 us (3%)
    pallas_call x1, Pallas kernels, body(): pl.pallas_call(kernel, out_shape=(jax.ShapeDtypeStruct((8, 48, 64), F32),...  132 us
    unnamed x8, local copies, waits for them, and re-layouts  4.47 us

profile of v1, /device:TPU:1, one launch (start us, length us, event | category | flops | bytes accessed | tf_op | source)
XLA Modules:
  0.0 136.6 jit_solution(14691824003566930443)
XLA Ops:
  0.6 1.4 %copy.12.fac_h = bf16[128,64]{1,0:T(8,128)(2,1)} copy(bf16[128,64]{0,1:T(8,128)(2,1)} %param.11) | data formatting | bytes 32768 | tf_op args[2]
  2.1 131.5 %shard_map.112 = (f32[8,48,64]{2,1,0:T(8,128)}, f32[8,48,64]{2,1,0:T(8,128)}, f32[64,64]{1,0:T(8,128)}) custom-call(s32[8]{0:T(128)} %order.1, bf16[8,384,128]{2,1,0:T(8,128)(2,1)} %data_h.1, bf16[128,64]{1,0:T(8,128)(2,1)} %copy.12.fac_h, f32[8,64]{1,0:T(8,128)} %w_h.1, f32[8,48,64]{2,1,0:T(8,128)} %aux_h.1, f32[8,48,64]{2,1,0:T(8,128)} %coup_h.1, ...), custom_call_target="tpu_custom_call" | custom-call | tf_op jit(solution)/shard_map/pallas_call | solution.py:364
  133.6 0.0 copy-start
  133.6 1.7 %copy.16 = f32[8,48,64]{2,1,0:T(8,128)} copy(f32[8,48,64]{2,1,0:T(8,128)} %get-tuple-element.6) | data formatting | bytes 196608
  135.3 0.0 copy-done
  135.3 0.0 copy-start.1
  135.3 0.7 copy.17
  135.9 0.1 copy-done.1
  136.0 0.6 copy.18
Async XLA Ops:
  133.6 1.7 %copy-start = (f32[8,48,64]{2,1,0:T(8,128)S(1)}, f32[8,48,64]{2,1,0:T(8,128)}, u32[]{:S(2)}) copy-start(f32[8,48,64]{2,1,0:T(8,128)} %get-tuple-element.7) | copy-start | bytes 294916
  135.3 0.8 copy-start.1

commit v2 on v1

v2 whole, which is shorter than its diff:
```python
import jax
import jax.numpy as jnp
from jax import lax
from jax.experimental import pallas as pl
from jax.experimental.pallas import tpu as pltpu
from jax.sharding import PartitionSpec as P

INNER = 3
POLAR = 8
NEWTON = 7
EPS_TRACE = 1e-06
F32 = jnp.float32
MESH = pl.DeviceIdType.MESH
CHEB_A = 0.1328125 / 1.2578125
CHEB_B = -1.0 / (512.0 * 1.2578125)


BF16 = jnp.bfloat16


def split(a):
    high = a.astype(BF16)
    return high, (a - high.astype(F32)).astype(BF16)


def lhs3(a):
    high, rest = split(a)
    return jnp.concatenate([high, rest, high], axis=1)


def dot(a, b):
    return jnp.dot(a, b, preferred_element_type=F32)


def gram_of(a, b):
    left, right = [], []
    for p, q in zip(a, b):
        ph, pl_ = split(p)
        qh, ql = split(q)
        left += [ph, pl_, ph]
        right += [qh, qh, ql]
    return lax.dot_general(
        jnp.concatenate(left, axis=0), jnp.concatenate(right, axis=0), (((0,), (0,)), ((), ())),
        preferred_element_type=F32,
    )


def kernel(
    order, data_h, fac_h, w_h, aux_h, coup_h, ds_h, dc_h, delta_h,
    evo_o, coup_o, delta_o,
    data_v, fac_v, w_v, aux_v, coup_v, ds_v, dc_v, delta_v,
    psend, precv, ysend, yrecv, fg, x_s, sys_s, x_rhs, cr, left_s, k_s,
    gsend, grecv, gall, ssend, srecv, sall, qsend, qrecv, zbuf, qall,
    aux_p, dss, talls, evos, us, at_s, baux, hal_a, hal_t, bsend, hal_b,
    load_sem, px_s, px_r, py_s, py_r, fg_s, fg_r,
    g1_s, g1_r, g2_s, g2_r, s1_s, s1_r, s2_s, s2_r, q1_s, q1_r, z_s, z_r, q2_s, q2_r, ha_s, ha_r, ht_s, ht_r, hb_s, hb_r,
):
    cuts = lax.axis_index("cuts")
    chan = lax.axis_index("chan")
    core = lax.rem(cuts, 2)
    zz = lax.rem(cuts // 2, 8)
    ylo = cuts // 16
    quad = ylo * 2 + core
    xx = lax.rem(chan, 4)
    yhi = chan // 4
    left_id = lax.rem(cuts + 31, 32)
    right_id = lax.rem(cuts + 1, 32)

    def z_dev(z):
        return (ylo * 16 + z * 2 + core, chan)

    def quad_dev(q):
        return ((q // 2) * 16 + zz * 2 + lax.rem(q, 2), chan)

    sent = []

    def send(src, dst, ssem, rsem, dev):
        copy = pltpu.make_async_remote_copy(
            src_ref=src, dst_ref=dst, send_sem=ssem, recv_sem=rsem, device_id=dev, device_id_type=MESH
        )
        copy.start()
        sent.append(copy)

    def arrived(dst, ssem, rsem):
        pltpu.make_async_remote_copy(
            src_ref=dst, dst_ref=dst, send_sem=ssem, recv_sem=rsem, device_id=(left_id, chan), device_id_type=MESH
        ).wait_recv()

    loads = []
    for n, (src, dst) in enumerate(
        (
            (fac_h, fac_v), (data_h, data_v), (w_h, w_v), (aux_h, aux_v), (coup_h, coup_v),
            (ds_h, ds_v), (dc_h, dc_v), (delta_h, delta_v),
        )
    ):
        copy = pltpu.make_async_copy(src, dst, load_sem.at[n])
        copy.start()
        loads.append(copy)

    barrier = pltpu.get_barrier_semaphore()
    greet = [(cuts, lax.rem(chan + d, 8)) for d in range(1, 8)]
    greet += [z_dev(lax.rem(zz + d, 8)) for d in range(1, 8)]
    greet += [quad_dev(lax.rem(quad + d, 4)) for d in range(1, 4)]
    greet += [(left_id, chan), (right_id, chan)]
    for dev in greet:
        pl.semaphore_signal(barrier, inc=1, device_id=dev, device_id_type=MESH)

    lane = lax.broadcasted_iota(jnp.int32, (1, 128), 1)
    low = lane < 64
    high = lane >= 64
    row_i = lax.broadcasted_iota(jnp.int32, (64, 128), 0)
    col_i = lax.broadcasted_iota(jnp.int32, (64, 128), 1)
    eye_b = row_i == lax.rem(col_i, 64)
    eye = eye_b.astype(F32)
    low16 = low.astype(F32).astype(BF16)
    high16 = high.astype(F32).astype(BF16)

    def swap(v):
        return pltpu.roll(v, 64, 1)

    def widen(v):
        return jnp.concatenate([v * low16, v * high16], axis=0)

    def rhs3(a):
        first, rest = split(a)
        first, rest = widen(first), widen(rest)
        return jnp.concatenate([first, first, rest], axis=0)

    def mm(a, b):
        return dot(lhs3(a), rhs3(b))

    def narrow(t):
        return jnp.where(low, t[0:64], t[64:128])

    def unpack(p):
        q = swap(p)
        return jnp.concatenate([jnp.where(low, p, q), jnp.where(low, q, p)], axis=0)

    def transposed(c):
        return jnp.concatenate([c, c], axis=0).T[0:64]

    def half_sums(v):
        zero = jnp.zeros_like(v)
        lo = jnp.sum(jnp.where(low, v, zero), axis=1, keepdims=True)
        hi = jnp.sum(jnp.where(low, zero, v), axis=1, keepdims=True)
        return jnp.where(low, lo, hi)

    loads[0].wait()
    fac = fac_v[...]
    partial_gram = lax.dot_general(fac, fac, (((0,), (0,)), ((), ())), preferred_element_type=F32)
    fg[chan] = jnp.concatenate([partial_gram[0:32], partial_gram[32:64]], axis=1)
    pl.semaphore_wait(barrier, len(greet))
    for d in range(1, 8):
        peer = lax.rem(chan + d, 8)
        send(fg.at[chan], fg.at[chan], fg_s.at[d - 1], fg_r.at[chan], (cuts, peer))

    zero_fac = jnp.zeros_like(fac)
    fac2 = jnp.concatenate(
        [jnp.concatenate([fac, zero_fac], axis=1), jnp.concatenate([zero_fac, fac], axis=1)], axis=0
    )
    loads[1].wait()
    for j in range(4):
        first = data_v[lax.rem(order[j], 8)]
        second = data_v[lax.rem(order[j + 4], 8)]
        out = jnp.dot(jnp.concatenate([first, second], axis=1), fac2, preferred_element_type=F32)
        for c in range(8):
            psend[c % 4, c // 4, j] = out[48 * c : 48 * c + 48]
    for d in (2, 1, 3):
        to = lax.rem(xx + d, 4)
        send(psend.at[to], precv.at[xx], px_s.at[d - 1], px_r.at[xx], (cuts, yhi * 4 + to))

    for n in range(2, 8):
        loads[n].wait()
    for j in range(4):
        aux_p[0, j] = jnp.concatenate([aux_v[j], aux_v[j + 4]], axis=1)
        dss[j] = jnp.concatenate([ds_v[j], ds_v[j + 4]], axis=1)
        dual = jnp.concatenate([dc_v[j], dc_v[j + 4]], axis=1)
        talls[j] = dual
        us[j] = jnp.concatenate([coup_v[j], coup_v[j + 4]], axis=1) - dual

    def halo_send(src, dst, ssem, rsem):
        send(src, dst.at[0], ssem.at[0], rsem.at[0], (right_id, chan))
        send(src, dst.at[1], ssem.at[1], rsem.at[1], (left_id, chan))

    halo_send(aux_p.at[0], hal_a.at[0], ha_s.at[0], ha_r.at[0])

    for d in range(1, 8):
        peer = lax.rem(chan + d, 8)
        arrived(fg.at[peer], fg_s.at[0], fg_r.at[peer])
    gram_sum = fg[0]
    for c in range(1, 8):
        gram_sum = gram_sum + fg[c]
    gram2 = unpack(gram_sum)
    w = w_v[...]
    w2 = jnp.concatenate([w[0:4], w[4:8]], axis=1)
    diag_row = jnp.sum(jnp.where(eye_b, gram2, 0.0), axis=0, keepdims=True)
    rho = half_sums(w2 * w2 * diag_row) * (1.0 / 64.0)
    w_over = w2 / rho
    b_rows = 2.0 / (rho + 4.0)
    a_rows = rho / (rho + 4.0)
    bsend[0:4] = b_rows
    bsend[4:8] = b_rows
    halo_send(bsend, hal_b, hb_s, hb_r)
    for j in range(4):
        w_col = half_sums(jnp.where(eye_b, w2[j : j + 1], 0.0))
        system = gram2 * w_col * w_over[j : j + 1] + 2.0 * eye
        sys_s[j] = lhs3(system)
        x_s[j] = CHEB_A * eye + CHEB_B * system

    def newton(step, carry):
        for j in range(4):
            x = x_s[j]
            x_s[j] = mm(x, 2.0 * eye - dot(sys_s[j], rhs3(x)))
        return carry

    lax.fori_loop(0, NEWTON, newton, 0)
    for j in range(4):
        x_rhs[j] = rhs3(x_s[j])

    for d in range(1, 4):
        frm = lax.rem(xx + d, 4)
        arrived(precv.at[frm], px_s.at[0], px_r.at[frm])
    for j in range(4):
        total = psend[xx, 1 - yhi, j]
        for d in range(1, 4):
            total = total + precv[lax.rem(xx + d, 4), 1 - yhi, j]
        ysend[j] = total
    send(ysend, yrecv, py_s, py_r, (cuts, (1 - yhi) * 4 + xx))
    for j in range(4):
        total = psend[xx, yhi, j]
        for d in range(1, 4):
            total = total + precv[lax.rem(xx + d, 4), yhi, j]
        baux[j] = total
    arrived(yrecv, py_s, py_r)
    for j in range(4):
        baux[j] = (baux[j] + yrecv[j]) * w_over[j : j + 1]

    delta_in = delta_v[...]
    delta = jnp.concatenate([delta_in, delta_in], axis=1)

    def spread(buf, ssem, rsem, own):
        buf[chan] = own
        for d in range(1, 8):
            peer = lax.rem(chan + d, 8)
            send(buf.at[chan], buf.at[chan], ssem.at[d - 1], rsem.at[chan], (cuts, peer))

    def from_chan(buf, ssem, rsem):
        for d in range(1, 8):
            peer = lax.rem(chan + d, 8)
            arrived(buf.at[peer], ssem.at[0], rsem.at[peer])

    def scatter(src, dst, ssem, rsem):
        for d in range(1, 8):
            peer = lax.rem(chan + d, 8)
            send(src.at[peer], dst.at[chan], ssem.at[d - 1], rsem.at[chan], (cuts, peer))
        dst[chan] = src[chan]

    def total_of(buf):
        total = buf[0]
        for c in range(1, 8):
            total = total + buf[c]
        return total

    def smooth(it):
        for n in range(2):
            arrived(hal_a.at[it, n], ha_s.at[it, n], ha_r.at[it, n])
            arrived(hal_t.at[it, n], ht_s.at[it, n], ht_r.at[it, n])
            if it == 0:
                arrived(hal_b.at[n], hb_s.at[n], hb_r.at[n])
        vals, tars, bs = [], [], []
        for p in range(4):
            vals.append(jnp.where(low, swap(hal_a[it, 0, p]), aux_p[it, p]))
            tars.append(jnp.where(low, swap(hal_t[it, 0, p]), at_s[it, p]))
            bs.append(jnp.where(low, swap(hal_b[0, p : p + 1]), bsend[p : p + 1]))
        for p in range(4):
            vals.append(jnp.where(low, aux_p[it, p], swap(hal_a[it, 1, p])))
            tars.append(jnp.where(low, at_s[it, p], swap(hal_t[it, 1, p])))
            bs.append(jnp.where(low, bsend[p : p + 1], swap(hal_b[1, p : p + 1])))
        for sweep in range(4):
            fresh = []
            for p in range(8):
                before = vals[p - 1] if p > 0 else swap(vals[7])
                after = vals[p + 1] if p < 7 else swap(vals[0])
                fresh.append(tars[p] + bs[p] * (before + after))
            vals = fresh
        for j in range(4):
            aux = jnp.where(low, vals[4 + j], vals[j])
            dual = dss[j] + evos[j] - aux
            if it == 0:
                aux_p[1, j] = aux
            dss[j] = dual
            us[j] = dot(lhs3(baux[j] + (aux - dual)), x_rhs[j])
        if it == 0:
            halo_send(aux_p.at[1], hal_a.at[1], ha_s.at[1], ha_r.at[1])
        for j in range(4):
            u, tall = us[j], talls[j]
            guu = narrow(gram_of([u], [u]))
            gtu = narrow(gram_of([tall], [u]))
            for h in range(2):
                ssend[it, 2 * j + h, 0] = guu[32 * h : 32 * h + 32]
                ssend[it, 2 * j + h, 1] = gtu[32 * h : 32 * h + 32]
        scatter(ssend.at[it], srecv.at[it], s1_s.at[it], s1_r.at[it])

    def gather_sums(it):
        from_chan(srecv.at[it], s1_s.at[it], s1_r.at[it])
        spread(sall.at[it], s2_s.at[it], s2_r.at[it], total_of(srecv.at[it]))

    def polar(step, carry):
        for j in range(4):
            both = cr[j]
            root = both[:, 128:256]
            ch, cl = split(both[:, 0:128])
            rh, rl = split(root)
            ch, cl = widen(ch), widen(cl)
            prod = dot(lhs3(root), jnp.concatenate([ch, ch, cl], axis=0))
            firsts = jnp.concatenate([ch, widen(rh)], axis=1)
            rests = jnp.concatenate([cl, widen(rl)], axis=1)
            bracket = 1.5 * eye - 0.5 * prod
            cr[j] = dot(lhs3(bracket), jnp.concatenate([firsts, firsts, rests], axis=0))
        return carry

    for j in range(4):
        dual = talls[j]
        evo = dot(lhs3(baux[j] + (aux_p[0, j] - dss[j]) + us[j]), x_rhs[j])
        tall = evo + dual
        evos[j] = evo
        talls[j] = tall
        part = narrow(gram_of([tall], [tall]))
        gsend[2 * j] = part[0:32]
        gsend[2 * j + 1] = part[32:64]
    scatter(gsend, grecv, g1_s, g1_r)
    for j in range(4):
        at_s[0, j] = (evos[j] + dss[j]) * a_rows[j : j + 1]
    halo_send(at_s.at[0], hal_t.at[0], ht_s.at[0], ht_r.at[0])
    from_chan(grecv, g1_s, g1_r)
    spread(gall, g2_s, g2_r, total_of(grecv))
    smooth(0)
    from_chan(gall, g2_s, g2_r)
    grams = [jnp.concatenate([gall[2 * j], gall[2 * j + 1]], axis=0) for j in range(4)]

    for it in range(INNER):
        last = it == INNER - 1
        delta_t = transposed(delta)
        delta_l = lhs3(delta)
        delta_r = rhs3(delta_t)
        scales = []
        for j in range(4):
            lefts = dot(delta_l, rhs3(grams[j]))
            left_s[j] = lefts
            normal = dot(lhs3(lefts), delta_r)
            trace = half_sums(jnp.sum(jnp.where(eye_b, normal, 0.0), axis=0, keepdims=True)) + EPS_TRACE
            scales.append(1.0 / jnp.sqrt(trace))
            cur = normal / trace
            bracket = 1.5 * eye - 0.5 * cur
            cr[j, :, 0:128] = mm(bracket, cur)
            cr[j, :, 128:256] = bracket

        if it == 0:
            lax.fori_loop(0, 3, polar, 0)
            gather_sums(0)
            lax.fori_loop(0, POLAR - 5, polar, 0)
        elif it == 1:
            lax.fori_loop(0, 2, polar, 0)
            smooth(1)
            lax.fori_loop(0, POLAR - 4, polar, 0)
        else:
            lax.fori_loop(0, POLAR - 2, polar, 0)
        part = jnp.zeros((64, 128), F32)
        for j in range(4):
            both = cr[j]
            root = both[:, 128:256]
            root = mm(1.5 * eye - 0.5 * mm(root, both[:, 0:128]), root)
            cr[j, :, 128:256] = root
            part = part + mm(root, left_s[j]) * scales[j]
        part = part + swap(part)
        packed = jnp.where(low, part[0:32], part[32:64])
        for q in range(4):
            qsend[it, q] = packed[8 * q : 8 * q + 8]
        for d in range(1, 4):
            to = lax.rem(quad + d, 4)
            send(qsend.at[it, to], qrecv.at[it, quad], q1_s.at[it, d - 1], q1_r.at[it, quad], quad_dev(to))
        qrecv[it, quad] = qsend[it, quad]
        if it == 1:
            gather_sums(1)
        delta_tl = lhs3(delta_t)
        for j in range(4):
            k_s[j] = dot(delta_tl, rhs3(cr[j, :, 128:256])) * scales[j]
        for d in range(1, 4):
            frm = lax.rem(quad + d, 4)
            arrived(qrecv.at[it, frm], q1_s.at[it, 0], q1_r.at[it, frm])
        zbuf[it, zz] = (qrecv[it, 0] + qrecv[it, 1]) + (qrecv[it, 2] + qrecv[it, 3])
        for d in range(1, 8):
            to = lax.rem(zz + d, 8)
            send(zbuf.at[it, zz], zbuf.at[it, zz], z_s.at[it, d - 1], z_r.at[it, zz], z_dev(to))
        for d in range(1, 8):
            frm = lax.rem(zz + d, 8)
            arrived(zbuf.at[it, frm], z_s.at[it, 0], z_r.at[it, frm])
        qall[it, quad] = total_of(zbuf.at[it]) * (1.0 / 256.0)
        for d in range(1, 4):
            to = lax.rem(quad + d, 4)
            send(qall.at[it, quad], qall.at[it, quad], q2_s.at[it, d - 1], q2_r.at[it, quad], quad_dev(to))
        if not last:
            from_chan(sall.at[it], s2_s.at[it], s2_r.at[it])
        for d in range(1, 4):
            frm = lax.rem(quad + d, 4)
            arrived(qall.at[it, frm], q2_s.at[it, 0], q2_r.at[it, frm])
        delta = unpack(jnp.concatenate([qall[it, q] for q in range(4)], axis=0))
        fresh_r = rhs3(delta)

        if last:
            for j in range(4):
                mixer = dot(lhs3(k_s[j]), fresh_r)
                coup = mm(talls[j], mixer)
                coup_o[j] = coup[:, 0:64]
                coup_o[j + 4] = coup[:, 64:128]
            delta_o[...] = delta[:, 0:64]
        else:
            fresh = []
            for j in range(4):
                mixer = dot(lhs3(k_s[j]), fresh_r)
                turn = dot(lhs3(2.0 * mixer - eye), x_rhs[j])
                tall = talls[j]
                both = dot(lhs3(tall), jnp.concatenate([rhs3(turn), rhs3(mixer)], axis=1))
                evo = us[j] + both[:, 0:128]
                evos[j] = evo
                talls[j] = evo + (tall - both[:, 128:256])
                if it == 0:
                    at_s[1, j] = (evo + dss[j]) * a_rows[j : j + 1]
                else:
                    evo_o[j] = evo[:, 0:64]
                    evo_o[j + 4] = evo[:, 64:128]
                step = turn + (eye - mixer)
                guu = jnp.concatenate([sall[it, 2 * j, 0], sall[it, 2 * j + 1, 0]], axis=0)
                gtu = jnp.concatenate([sall[it, 2 * j, 1], sall[it, 2 * j + 1, 1]], axis=0)
                side = gtu + 0.5 * mm(grams[j], step)
                fresh.append(guu + narrow(gram_of([step, side], [side, step])))
            if it == 0:
                halo_send(at_s.at[1], hal_t.at[1], ht_s.at[1], ht_r.at[1])
            grams = fresh

    for copy in sent:
        copy.wait_send()


def body(data, order, chan_factor, slice_weights, smooth_aux, coupled, smooth_dual, coupling_dual, delta):
    vm = pltpu.VMEM
    dma = pltpu.SemaphoreType.DMA
    rows = (4, 48, 128)
    anyspace = pl.BlockSpec(memory_space=pl.ANY)
    vspace = pl.BlockSpec(memory_space=pltpu.VMEM)
    return pl.pallas_call(
        kernel,
        out_shape=(
            jax.ShapeDtypeStruct((8, 48, 64), F32),
            jax.ShapeDtypeStruct((8, 48, 64), F32),
            jax.ShapeDtypeStruct((64, 64), F32),
        ),
        in_specs=[pl.BlockSpec(memory_space=pltpu.SMEM)] + [anyspace] * 8,
        out_specs=(vspace, vspace, vspace),
        scratch_shapes=[
            vm((8, 384, 128), jnp.bfloat16), vm((128, 64), jnp.bfloat16), vm((8, 64), F32),
            vm((8, 48, 64), F32), vm((8, 48, 64), F32), vm((8, 48, 64), F32), vm((8, 48, 64), F32), vm((64, 64), F32),
            vm((4, 2) + rows, F32), vm((4, 2) + rows, F32), vm(rows, F32), vm(rows, F32),
            vm((8, 32, 128), F32), vm((4, 64, 128), F32), vm((4, 64, 384), BF16), vm((4, 384, 128), BF16),
            vm((4, 64, 256), F32), vm((4, 64, 128), F32), vm((4, 64, 128), F32),
            vm((8, 32, 128), F32), vm((8, 32, 128), F32), vm((8, 32, 128), F32),
            vm((2, 8, 2, 32, 128), F32), vm((2, 8, 2, 32, 128), F32), vm((2, 8, 2, 32, 128), F32),
            vm((3, 4, 8, 128), F32), vm((3, 4, 8, 128), F32), vm((3, 8, 8, 128), F32), vm((3, 4, 8, 128), F32),
            vm((2,) + rows, F32), vm(rows, F32), vm(rows, F32), vm(rows, F32), vm(rows, F32),
            vm((2,) + rows, F32), vm(rows, F32),
            vm((2, 2) + rows, F32), vm((2, 2) + rows, F32), vm((8, 128), F32), vm((2, 8, 128), F32),
            dma((8,)), dma((3,)), dma((4,)), dma, dma, dma((7,)), dma((8,)),
            dma((7,)), dma((8,)), dma((7,)), dma((8,)),
            dma((2, 7)), dma((2, 8)), dma((2, 7)), dma((2, 8)),
            dma((3, 3)), dma((3, 4)), dma((3, 7)), dma((3, 8)), dma((3, 3)), dma((3, 4)),
            dma((2, 2)), dma((2, 2)), dma((2, 2)), dma((2, 2)), dma((2,)), dma((2,)),
        ],
        compiler_params=pltpu.CompilerParams(
            collective_id=0, has_side_effects=True, vmem_limit_bytes=60 * 1024 * 1024
        ),
    )(order, data, chan_factor, slice_weights, smooth_aux, coupled, smooth_dual, coupling_dual, delta)


def solution(mesh):
    return jax.shard_map(
        body,
        mesh=mesh,
        in_specs=(
            P("cuts", None, "chan"),
            P("cuts"),
            P("chan", None),
            P("cuts", None),
            P("cuts", "chan", None),
            P("cuts", "chan", None),
            P("cuts", "chan", None),
            P("cuts", "chan", None),
            P(),
        ),
        out_specs=(P("cuts", "chan", None), P("cuts", "chan", None), P()),
        check_vma=False,
    )
```

time: 137 us -> 105 us (0.77)
  Pallas kernels: 132 us -> 100 us
    pallas_call x1, Pallas kernels: 132 us -> 100 us  [body(): pl.pallas_call(kernel, out_shape=(jax.ShapeDtypeStruct((8, 48, 64), F32),...]
where the time goes in v2:
time: 105 us
  Pallas kernels  100 us (95%)
  local copies, waits for them, and re-layouts  4.47 us (4%)
    pallas_call x1, Pallas kernels, body(): pl.pallas_call(kernel, out_shape=(jax.ShapeDtypeStruct((8, 48, 64), F32),...  100 us
    unnamed x8, local copies, waits for them, and re-layouts  4.47 us

profile of v2, /device:TPU:1, one launch (start us, length us, event | category | flops | bytes accessed | tf_op | source)
XLA Modules:
  0.0 105.1 jit_solution(7736046558914584891)
XLA Ops:
  0.6 1.4 %copy.12.fac_h = bf16[128,64]{1,0:T(8,128)(2,1)} copy(bf16[128,64]{0,1:T(8,128)(2,1)} %param.11) | data formatting | bytes 32768 | tf_op args[2]
  2.1 100.0 %shard_map.112 = (f32[8,48,64]{2,1,0:T(8,128)}, f32[8,48,64]{2,1,0:T(8,128)}, f32[64,64]{1,0:T(8,128)}) custom-call(s32[8]{0:T(128)} %order.1, bf16[8,384,128]{2,1,0:T(8,128)(2,1)} %data_h.1, bf16[128,64]{1,0:T(8,128)(2,1)} %copy.12.fac_h, f32[8,64]{1,0:T(8,128)} %w_h.1, f32[8,48,64]{2,1,0:T(8,128)} %aux_h.1, f32[8,48,64]{2,1,0:T(8,128)} %coup_h.1, ...), custom_call_target="tpu_custom_call" | custom-call | tf_op jit(solution)/shard_map/pallas_call | solution.py:451
  102.1 0.0 copy-start
  102.1 1.7 %copy.16 = f32[8,48,64]{2,1,0:T(8,128)} copy(f32[8,48,64]{2,1,0:T(8,128)} %get-tuple-element.6) | data formatting | bytes 196608
  103.8 0.0 copy-done
  103.8 0.0 copy-start.1
  103.8 0.7 copy.17
  104.5 0.1 copy-done.1
  104.5 0.6 copy.18
Async XLA Ops:
  102.1 1.7 %copy-start = (f32[8,48,64]{2,1,0:T(8,128)S(1)}, f32[8,48,64]{2,1,0:T(8,128)}, u32[]{:S(2)}) copy-start(f32[8,48,64]{2,1,0:T(8,128)} %get-tuple-element.7) | copy-start | bytes 294916
  103.8 0.8 copy-start.1

commit v3 on v2

--- a/solution.py
+++ b/solution.py
@@ -48,12 +48,12 @@
 def kernel(
     order, data_h, fac_h, w_h, aux_h, coup_h, ds_h, dc_h, delta_h,
     evo_o, coup_o, delta_o,
-    data_v, fac_v, w_v, aux_v, coup_v, ds_v, dc_v, delta_v,
+    data_v, fac_v, w_v, rows_v, delta_v,
     psend, precv, ysend, yrecv, fg, x_s, sys_s, x_rhs, cr, left_s, k_s,
     gsend, grecv, gall, ssend, srecv, sall, qsend, qrecv, zbuf, qall,
-    aux_p, dss, talls, evos, us, at_s, baux, hal_a, hal_t, bsend, hal_b,
-    load_sem, px_s, px_r, py_s, py_r, fg_s, fg_r,
-    g1_s, g1_r, g2_s, g2_r, s1_s, s1_r, s2_s, s2_r, q1_s, q1_r, z_s, z_r, q2_s, q2_r, ha_s, ha_r, ht_s, ht_r, hb_s, hb_r,
+    aux_p, dss, talls, evos, us, mix_s, at_s, baux, hal_a, hal_t, bsend, hal_b,
+    load_sem, px_s, px_r, py_s, py_r, fg_s, fg_r, g1_s, g1_r, g2_s, g2_r, s1_s, s1_r, s2_s, s2_r,
+    q1_s, q1_r, z_s, z_r, q2_s, q2_r, ha_s, ha_r, ht_s, ht_r, hb_s, hb_r,
 ):
     cuts = lax.axis_index("cuts")
     chan = lax.axis_index("chan")
@@ -72,30 +72,28 @@
     def quad_dev(q):
         return ((q // 2) * 16 + zz * 2 + lax.rem(q, 2), chan)
 
-    sent = []
-
     def send(src, dst, ssem, rsem, dev):
-        copy = pltpu.make_async_remote_copy(
+        pltpu.make_async_remote_copy(
             src_ref=src, dst_ref=dst, send_sem=ssem, recv_sem=rsem, device_id=dev, device_id_type=MESH
+        ).start()
+
+    def whole(ref, ssem, rsem):
+        return pltpu.make_async_remote_copy(
+            src_ref=ref, dst_ref=ref, send_sem=ssem, recv_sem=rsem, device_id=(left_id, chan), device_id_type=MESH
         )
-        copy.start()
-        sent.append(copy)
-
-    def arrived(dst, ssem, rsem):
-        pltpu.make_async_remote_copy(
-            src_ref=dst, dst_ref=dst, send_sem=ssem, recv_sem=rsem, device_id=(left_id, chan), device_id_type=MESH
-        ).wait_recv()
-
-    loads = []
-    for n, (src, dst) in enumerate(
-        (
-            (fac_h, fac_v), (data_h, data_v), (w_h, w_v), (aux_h, aux_v), (coup_h, coup_v),
-            (ds_h, ds_v), (dc_h, dc_v), (delta_h, delta_v),
-        )
-    ):
-        copy = pltpu.make_async_copy(src, dst, load_sem.at[n])
-        copy.start()
-        loads.append(copy)
+
+    def arrived(ref, ssem, rsem):
+        whole(ref, ssem, rsem).wait_recv()
+
+    def load(src, dst, n):
+        return pltpu.make_async_copy(src, dst, load_sem.at[n])
+
+    load(fac_h, fac_v, 0).start()
+    load(data_h, data_v, 1).start()
+    load(w_h, w_v, 2).start()
+    for n, src in enumerate((aux_h, coup_h, ds_h, dc_h)):
+        load(src, rows_v.at[n], 3).start()
+    load(delta_h, delta_v, 4).start()
 
     barrier = pltpu.get_barrier_semaphore()
     greet = [(cuts, lax.rem(chan + d, 8)) for d in range(1, 8)]
@@ -145,48 +143,52 @@
         hi = jnp.sum(jnp.where(low, zero, v), axis=1, keepdims=True)
         return jnp.where(low, lo, hi)
 
-    loads[0].wait()
+    load(fac_h, fac_v, 0).wait()
     fac = fac_v[...]
-    partial_gram = lax.dot_general(fac, fac, (((0,), (0,)), ((), ())), preferred_element_type=F32)
+    nt = (((1,), (1,)), ((), ()))
+    partial_gram = lax.dot_general(fac, fac, nt, preferred_element_type=F32)
     fg[chan] = jnp.concatenate([partial_gram[0:32], partial_gram[32:64]], axis=1)
     pl.semaphore_wait(barrier, len(greet))
     for d in range(1, 8):
         peer = lax.rem(chan + d, 8)
-        send(fg.at[chan], fg.at[chan], fg_s.at[d - 1], fg_r.at[chan], (cuts, peer))
+        send(fg.at[chan], fg.at[chan], fg_s, fg_r, (cuts, peer))
 
     zero_fac = jnp.zeros_like(fac)
     fac2 = jnp.concatenate(
         [jnp.concatenate([fac, zero_fac], axis=1), jnp.concatenate([zero_fac, fac], axis=1)], axis=0
     )
-    loads[1].wait()
+    load(data_h, data_v, 1).wait()
     for j in range(4):
         first = data_v[lax.rem(order[j], 8)]
         second = data_v[lax.rem(order[j + 4], 8)]
-        out = jnp.dot(jnp.concatenate([first, second], axis=1), fac2, preferred_element_type=F32)
+        out = lax.dot_general(jnp.concatenate([first, second], axis=1), fac2, nt, preferred_element_type=F32)
         for c in range(8):
-            psend[c % 4, c // 4, j] = out[48 * c : 48 * c + 48]
-    for d in (2, 1, 3):
-        to = lax.rem(xx + d, 4)
-        send(psend.at[to], precv.at[xx], px_s.at[d - 1], px_r.at[xx], (cuts, yhi * 4 + to))
-
-    for n in range(2, 8):
-        loads[n].wait()
+            psend[j, c % 4, c // 4] = out[48 * c : 48 * c + 48]
+        for d in (2, 1, 3):
+            to = lax.rem(xx + d, 4)
+            send(psend.at[j, to], precv.at[j, xx], px_s, px_r.at[j], (cuts, yhi * 4 + to))
+
+    load(w_h, w_v, 2).wait()
+    load(rows_v, rows_v, 3).wait()
+    load(delta_h, delta_v, 4).wait()
+
+    def pair(n, j):
+        return jnp.concatenate([rows_v[n, j], rows_v[n, j + 4]], axis=1)
+
     for j in range(4):
-        aux_p[0, j] = jnp.concatenate([aux_v[j], aux_v[j + 4]], axis=1)
-        dss[j] = jnp.concatenate([ds_v[j], ds_v[j + 4]], axis=1)
-        dual = jnp.concatenate([dc_v[j], dc_v[j + 4]], axis=1)
+        aux_p[0, j] = pair(0, j)
+        dss[j] = pair(2, j)
+        dual = pair(3, j)
         talls[j] = dual
-        us[j] = jnp.concatenate([coup_v[j], coup_v[j + 4]], axis=1) - dual
+        us[j] = pair(1, j) - dual
 
     def halo_send(src, dst, ssem, rsem):
-        send(src, dst.at[0], ssem.at[0], rsem.at[0], (right_id, chan))
-        send(src, dst.at[1], ssem.at[1], rsem.at[1], (left_id, chan))
-
-    halo_send(aux_p.at[0], hal_a.at[0], ha_s.at[0], ha_r.at[0])
-
-    for d in range(1, 8):
-        peer = lax.rem(chan + d, 8)
-        arrived(fg.at[peer], fg_s.at[0], fg_r.at[peer])
+        send(src, dst.at[0], ssem, rsem, (right_id, chan))
+        send(src, dst.at[1], ssem, rsem, (left_id, chan))
+
+    halo_send(aux_p.at[0], hal_a.at[0], ha_s, ha_r.at[0])
+
+    arrived(fg.at[pl.ds(0, 7)], fg_s, fg_r)
     gram_sum = fg[0]
     for c in range(1, 8):
         gram_sum = gram_sum + fg[c]
@@ -213,27 +215,27 @@
             x_s[j] = mm(x, 2.0 * eye - dot(sys_s[j], rhs3(x)))
         return carry
 
-    lax.fori_loop(0, NEWTON, newton, 0)
+    def forward(j):
+        arrived(precv.at[j, pl.ds(0, 3)], px_s, px_r.at[j])
+        total = psend[j, xx, 1 - yhi]
+        for d in range(1, 4):
+            total = total + precv[j, lax.rem(xx + d, 4), 1 - yhi]
+        ysend[j] = total
+        send(ysend.at[j], yrecv.at[j], py_s, py_r.at[j], (cuts, (1 - yhi) * 4 + xx))
+        total = psend[j, xx, yhi]
+        for d in range(1, 4):
+            total = total + precv[j, lax.rem(xx + d, 4), yhi]
+        baux[j] = total
+
+    lax.fori_loop(0, 2, newton, 0)
+    forward(0)
+    lax.fori_loop(0, 3, newton, 0)
+    forward(1)
+    lax.fori_loop(0, NEWTON - 5, newton, 0)
+    forward(2)
     for j in range(4):
         x_rhs[j] = rhs3(x_s[j])
-
-    for d in range(1, 4):
-        frm = lax.rem(xx + d, 4)
-        arrived(precv.at[frm], px_s.at[0], px_r.at[frm])
-    for j in range(4):
-        total = psend[xx, 1 - yhi, j]
-        for d in range(1, 4):
-            total = total + precv[lax.rem(xx + d, 4), 1 - yhi, j]
-        ysend[j] = total
-    send(ysend, yrecv, py_s, py_r, (cuts, (1 - yhi) * 4 + xx))
-    for j in range(4):
-        total = psend[xx, yhi, j]
-        for d in range(1, 4):
-            total = total + precv[lax.rem(xx + d, 4), yhi, j]
-        baux[j] = total
-    arrived(yrecv, py_s, py_r)
-    for j in range(4):
-        baux[j] = (baux[j] + yrecv[j]) * w_over[j : j + 1]
+    forward(3)
 
     delta_in = delta_v[...]
     delta = jnp.concatenate([delta_in, delta_in], axis=1)
@@ -241,19 +243,16 @@
     def spread(buf, ssem, rsem, own):
         buf[chan] = own
         for d in range(1, 8):
-            peer = lax.rem(chan + d, 8)
-            send(buf.at[chan], buf.at[chan], ssem.at[d - 1], rsem.at[chan], (cuts, peer))
-
-    def from_chan(buf, ssem, rsem):
-        for d in range(1, 8):
-            peer = lax.rem(chan + d, 8)
-            arrived(buf.at[peer], ssem.at[0], rsem.at[peer])
+            send(buf.at[chan], buf.at[chan], ssem, rsem, (cuts, lax.rem(chan + d, 8)))
 
     def scatter(src, dst, ssem, rsem):
         for d in range(1, 8):
             peer = lax.rem(chan + d, 8)
-            send(src.at[peer], dst.at[chan], ssem.at[d - 1], rsem.at[chan], (cuts, peer))
+            send(src.at[peer], dst.at[chan], ssem, rsem, (cuts, peer))
         dst[chan] = src[chan]
+
+    def from_chan(buf, ssem, rsem):
+        arrived(buf.at[pl.ds(0, 7)], ssem, rsem)
 
     def total_of(buf):
         total = buf[0]
@@ -262,11 +261,10 @@
         return total
 
     def smooth(it):
-        for n in range(2):
-            arrived(hal_a.at[it, n], ha_s.at[it, n], ha_r.at[it, n])
-            arrived(hal_t.at[it, n], ht_s.at[it, n], ht_r.at[it, n])
-            if it == 0:
-                arrived(hal_b.at[n], hb_s.at[n], hb_r.at[n])
+        arrived(hal_a.at[it], ha_s, ha_r.at[it])
+        arrived(hal_t.at[it], ht_s, ht_r.at[it])
+        if it == 0:
+            arrived(hal_b, hb_s, hb_r)
         vals, tars, bs = [], [], []
         for p in range(4):
             vals.append(jnp.where(low, swap(hal_a[it, 0, p]), aux_p[it, p]))
@@ -291,7 +289,7 @@
             dss[j] = dual
             us[j] = dot(lhs3(baux[j] + (aux - dual)), x_rhs[j])
         if it == 0:
-            halo_send(aux_p.at[1], hal_a.at[1], ha_s.at[1], ha_r.at[1])
+            halo_send(aux_p.at[1], hal_a.at[1], ha_s, ha_r.at[1])
         for j in range(4):
             u, tall = us[j], talls[j]
             guu = narrow(gram_of([u], [u]))
@@ -299,11 +297,17 @@
             for h in range(2):
                 ssend[it, 2 * j + h, 0] = guu[32 * h : 32 * h + 32]
                 ssend[it, 2 * j + h, 1] = gtu[32 * h : 32 * h + 32]
-        scatter(ssend.at[it], srecv.at[it], s1_s.at[it], s1_r.at[it])
+        scatter(ssend.at[it], srecv.at[it], s1_s, s1_r.at[it])
 
     def gather_sums(it):
-        from_chan(srecv.at[it], s1_s.at[it], s1_r.at[it])
-        spread(sall.at[it], s2_s.at[it], s2_r.at[it], total_of(srecv.at[it]))
+        from_chan(srecv.at[it], s1_s, s1_r.at[it])
+        spread(sall.at[it], s2_s, s2_r.at[it], total_of(srecv.at[it]))
+
+    def rows_of(j):
+        tall = talls[j]
+        both = dot(lhs3(tall), mix_s[j])
+        evo = us[j] + both[:, 0:128]
+        return evo, evo + (tall - both[:, 128:256])
 
     def polar(step, carry):
         for j in range(4):
@@ -320,6 +324,8 @@
         return carry
 
     for j in range(4):
+        arrived(yrecv.at[j], py_s, py_r.at[j])
+        baux[j] = (baux[j] + yrecv[j]) * w_over[j : j + 1]
         dual = talls[j]
         evo = dot(lhs3(baux[j] + (aux_p[0, j] - dss[j]) + us[j]), x_rhs[j])
         tall = evo + dual
@@ -331,7 +337,7 @@
     scatter(gsend, grecv, g1_s, g1_r)
     for j in range(4):
         at_s[0, j] = (evos[j] + dss[j]) * a_rows[j : j + 1]
-    halo_send(at_s.at[0], hal_t.at[0], ht_s.at[0], ht_r.at[0])
+    halo_send(at_s.at[0], hal_t.at[0], ht_s, ht_r.at[0])
     from_chan(grecv, g1_s, g1_r)
     spread(gall, g2_s, g2_r, total_of(grecv))
     smooth(0)
@@ -375,36 +381,39 @@
         part = part + swap(part)
         packed = jnp.where(low, part[0:32], part[32:64])
         for q in range(4):
-            qsend[it, q] = packed[8 * q : 8 * q + 8]
+            qsend[it * 4 + q] = packed[8 * q : 8 * q + 8]
         for d in range(1, 4):
             to = lax.rem(quad + d, 4)
-            send(qsend.at[it, to], qrecv.at[it, quad], q1_s.at[it, d - 1], q1_r.at[it, quad], quad_dev(to))
-        qrecv[it, quad] = qsend[it, quad]
+            send(qsend.at[it * 4 + to], qrecv.at[it, quad], q1_s, q1_r.at[it], quad_dev(to))
+        qrecv[it, quad] = qsend[it * 4 + quad]
         if it == 1:
             gather_sums(1)
         delta_tl = lhs3(delta_t)
         for j in range(4):
             k_s[j] = dot(delta_tl, rhs3(cr[j, :, 128:256])) * scales[j]
+        arrived(qrecv.at[it, pl.ds(0, 3)], q1_s, q1_r.at[it])
+        zbuf[it * 8 + zz] = (qrecv[it, 0] + qrecv[it, 1]) + (qrecv[it, 2] + qrecv[it, 3])
+        for d in (4, 3, 5, 2, 6, 1, 7):
+            slot = zbuf.at[it * 8 + zz]
+            send(slot, slot, z_s, z_r.at[it], z_dev(lax.rem(zz + d, 8)))
+        if last:
+            for j in range(4):
+                evo, tall = rows_of(j)
+                talls[j] = tall
+                evo_o[j] = evo[:, 0:64]
+                evo_o[j + 4] = evo[:, 64:128]
+        arrived(zbuf.at[pl.ds(it * 8, 7)], z_s, z_r.at[it])
+        total = zbuf[it * 8]
+        for z in range(1, 8):
+            total = total + zbuf[it * 8 + z]
+        qall[it * 4 + quad] = total * (1.0 / 256.0)
         for d in range(1, 4):
-            frm = lax.rem(quad + d, 4)
-            arrived(qrecv.at[it, frm], q1_s.at[it, 0], q1_r.at[it, frm])
-        zbuf[it, zz] = (qrecv[it, 0] + qrecv[it, 1]) + (qrecv[it, 2] + qrecv[it, 3])
-        for d in range(1, 8):
-            to = lax.rem(zz + d, 8)
-            send(zbuf.at[it, zz], zbuf.at[it, zz], z_s.at[it, d - 1], z_r.at[it, zz], z_dev(to))
-        for d in range(1, 8):
-            frm = lax.rem(zz + d, 8)
-            arrived(zbuf.at[it, frm], z_s.at[it, 0], z_r.at[it, frm])
-        qall[it, quad] = total_of(zbuf.at[it]) * (1.0 / 256.0)
-        for d in range(1, 4):
-            to = lax.rem(quad + d, 4)
-            send(qall.at[it, quad], qall.at[it, quad], q2_s.at[it, d - 1], q2_r.at[it, quad], quad_dev(to))
+            slot = qall.at[it * 4 + quad]
+            send(slot, slot, q2_s, q2_r.at[it], quad_dev(lax.rem(quad + d, 4)))
         if not last:
-            from_chan(sall.at[it], s2_s.at[it], s2_r.at[it])
-        for d in range(1, 4):
-            frm = lax.rem(quad + d, 4)
-            arrived(qall.at[it, frm], q2_s.at[it, 0], q2_r.at[it, frm])
-        delta = unpack(jnp.concatenate([qall[it, q] for q in range(4)], axis=0))
+            from_chan(sall.at[it], s2_s, s2_r.at[it])
+        arrived(qall.at[pl.ds(it * 4, 3)], q2_s, q2_r.at[it])
+        delta = unpack(jnp.concatenate([qall[it * 4 + q] for q in range(4)], axis=0))
         fresh_r = rhs3(delta)
 
         if last:
@@ -419,27 +428,38 @@
             for j in range(4):
                 mixer = dot(lhs3(k_s[j]), fresh_r)
                 turn = dot(lhs3(2.0 * mixer - eye), x_rhs[j])
-                tall = talls[j]
-                both = dot(lhs3(tall), jnp.concatenate([rhs3(turn), rhs3(mixer)], axis=1))
-                evo = us[j] + both[:, 0:128]
-                evos[j] = evo
-                talls[j] = evo + (tall - both[:, 128:256])
+                mix_s[j, :, 0:128] = rhs3(turn)
+                mix_s[j, :, 128:256] = rhs3(mixer)
                 if it == 0:
+                    evo, tall = rows_of(j)
+                    evos[j] = evo
+                    talls[j] = tall
                     at_s[1, j] = (evo + dss[j]) * a_rows[j : j + 1]
-                else:
-                    evo_o[j] = evo[:, 0:64]
-                    evo_o[j + 4] = evo[:, 64:128]
                 step = turn + (eye - mixer)
                 guu = jnp.concatenate([sall[it, 2 * j, 0], sall[it, 2 * j + 1, 0]], axis=0)
                 gtu = jnp.concatenate([sall[it, 2 * j, 1], sall[it, 2 * j + 1, 1]], axis=0)
                 side = gtu + 0.5 * mm(grams[j], step)
                 fresh.append(guu + narrow(gram_of([step, side], [side, step])))
             if it == 0:
-                halo_send(at_s.at[1], hal_t.at[1], ht_s.at[1], ht_r.at[1])
+                halo_send(at_s.at[1], hal_t.at[1], ht_s, ht_r.at[1])
             grams = fresh
 
-    for copy in sent:
-        copy.wait_send()
+    for ref, ssem, rsem in (
+        (psend.at[pl.ds(0, 3)], px_s, px_r.at[0]),
+        (ysend, py_s, py_r.at[0]),
+        (fg.at[pl.ds(0, 7)], fg_s, fg_r),
+        (gsend.at[pl.ds(0, 7)], g1_s, g1_r),
+        (gall.at[pl.ds(0, 7)], g2_s, g2_r),
+        (ssend.at[:, pl.ds(0, 7)], s1_s, s1_r.at[0]),
+        (sall.at[:, pl.ds(0, 7)], s2_s, s2_r.at[0]),
+        (qsend.at[pl.ds(0, 9)], q1_s, q1_r.at[0]),
+        (zbuf.at[pl.ds(0, 21)], z_s, z_r.at[0]),
+        (qall.at[pl.ds(0, 9)], q2_s, q2_r.at[0]),
+        (hal_a, ha_s, ha_r.at[0]),
+        (hal_t, ht_s, ht_r.at[0]),
+        (hal_b, hb_s, hb_r),
+    ):
+        whole(ref, ssem, rsem).wait_send()
 
 
 def body(data, order, chan_factor, slice_weights, smooth_aux, coupled, smooth_dual, coupling_dual, delta):
@@ -458,27 +478,23 @@
         in_specs=[pl.BlockSpec(memory_space=pltpu.SMEM)] + [anyspace] * 8,
         out_specs=(vspace, vspace, vspace),
         scratch_shapes=[
-            vm((8, 384, 128), jnp.bfloat16), vm((128, 64), jnp.bfloat16), vm((8, 64), F32),
-            vm((8, 48, 64), F32), vm((8, 48, 64), F32), vm((8, 48, 64), F32), vm((8, 48, 64), F32), vm((64, 64), F32),
-            vm((4, 2) + rows, F32), vm((4, 2) + rows, F32), vm(rows, F32), vm(rows, F32),
+            vm((8, 384, 128), BF16), vm((64, 128), BF16), vm((8, 64), F32), vm((4, 8, 48, 64), F32), vm((64, 64), F32),
+            vm((4, 4, 2, 48, 128), F32), vm((4, 4, 2, 48, 128), F32), vm(rows, F32), vm(rows, F32),
             vm((8, 32, 128), F32), vm((4, 64, 128), F32), vm((4, 64, 384), BF16), vm((4, 384, 128), BF16),
             vm((4, 64, 256), F32), vm((4, 64, 128), F32), vm((4, 64, 128), F32),
             vm((8, 32, 128), F32), vm((8, 32, 128), F32), vm((8, 32, 128), F32),
             vm((2, 8, 2, 32, 128), F32), vm((2, 8, 2, 32, 128), F32), vm((2, 8, 2, 32, 128), F32),
-            vm((3, 4, 8, 128), F32), vm((3, 4, 8, 128), F32), vm((3, 8, 8, 128), F32), vm((3, 4, 8, 128), F32),
-            vm((2,) + rows, F32), vm(rows, F32), vm(rows, F32), vm(rows, F32), vm(rows, F32),
+            vm((12, 8, 128), F32), vm((3, 4, 8, 128), F32), vm((24, 8, 128), F32), vm((12, 8, 128), F32),
+            vm((2,) + rows, F32), vm(rows, F32), vm(rows, F32), vm(rows, F32), vm(rows, F32), vm((4, 384, 256), BF16),
             vm((2,) + rows, F32), vm(rows, F32),
             vm((2, 2) + rows, F32), vm((2, 2) + rows, F32), vm((8, 128), F32), vm((2, 8, 128), F32),
-            dma((8,)), dma((3,)), dma((4,)), dma, dma, dma((7,)), dma((8,)),
-            dma((7,)), dma((8,)), dma((7,)), dma((8,)),
-            dma((2, 7)), dma((2, 8)), dma((2, 7)), dma((2, 8)),
-            dma((3, 3)), dma((3, 4)), dma((3, 7)), dma((3, 8)), dma((3, 3)), dma((3, 4)),
-            dma((2, 2)), dma((2, 2)), dma((2, 2)), dma((2, 2)), dma((2,)), dma((2,)),
+            dma((5,)), dma, dma((4,)), dma, dma((4,)), dma, dma, dma, dma, dma, dma, dma, dma((2,)), dma, dma((2,)),
+            dma, dma((3,)), dma, dma((3,)), dma, dma((3,)), dma, dma((2,)), dma, dma((2,)), dma, dma,
         ],
         compiler_params=pltpu.CompilerParams(
             collective_id=0, has_side_effects=True, vmem_limit_bytes=60 * 1024 * 1024
         ),
-    )(order, data, chan_factor, slice_weights, smooth_aux, coupled, smooth_dual, coupling_dual, delta)
+    )(order, data, chan_factor.T, slice_weights, smooth_aux, coupled, smooth_dual, coupling_dual, delta)
 
 
 def solution(mesh):

time: 105 us -> 98.2 us (0.935)
  Pallas kernels: 100 us -> 94.3 us
  local copies, waits for them, and re-layouts: 4.47 us -> 3.03 us
    pallas_call x1, Pallas kernels: 100 us -> 94.3 us  [body(): pl.pallas_call(kernel, out_shape=(jax.ShapeDtypeStruct((8, 48, 64), F32),...]
    unnamed x8 -> x7, local copies, waits for them, and re-layouts: 4.47 us -> 3.03 us
where the time goes in v3:
time: 98.2 us; the launch traced here: 98 us
  Pallas kernels  94.3 us (96%)
  local copies, waits for them, and re-layouts  3.03 us (3%)
    pallas_call x1, Pallas kernels, body(): pl.pallas_call(kernel, out_shape=(jax.ShapeDtypeStruct((8, 48, 64), F32),...  94.3 us
    unnamed x7, local copies, waits for them, and re-layouts  3.03 us

profile of v3, /device:TPU:1, one launch (start us, length us, event | category | flops | bytes accessed | tf_op | source)
XLA Modules:
  0.0 98.0 jit_solution(9419461178003507427)
XLA Ops:
  0.6 94.3 %shard_map.112 = (f32[8,48,64]{2,1,0:T(8,128)}, f32[8,48,64]{2,1,0:T(8,128)}, f32[64,64]{1,0:T(8,128)}) custom-call(s32[8]{0:T(128)} %order.1, bf16[8,384,128]{2,1,0:T(8,128)(2,1)} %data_h.1, bf16[64,128]{1,0:T(8,128)(2,1)} %bitcast.1, f32[8,64]{1,0:T(8,128)} %w_h.1, f32[8,48,64]{2,1,0:T(8,128)} %aux_h.1, f32[8,48,64]{2,1,0:T(8,128)} %coup_h.1, ...), custom_call_target="tpu_custom_call" | custom-call | tf_op jit(solution)/shard_map/pallas_call | solution.py:471
  94.9 0.0 copy-start
  94.9 1.7 %copy.15 = f32[8,48,64]{2,1,0:T(8,128)} copy(f32[8,48,64]{2,1,0:T(8,128)} %get-tuple-element.6) | data formatting | bytes 196608
  96.6 0.0 copy-done
  96.6 0.0 copy-start.1
  96.6 0.7 copy.16
  97.3 0.1 copy-done.1
  97.4 0.6 copy.17
Async XLA Ops:
  94.9 1.7 %copy-start = (f32[8,48,64]{2,1,0:T(8,128)S(1)}, f32[8,48,64]{2,1,0:T(8,128)}, u32[]{:S(2)}) copy-start(f32[8,48,64]{2,1,0:T(8,128)} %get-tuple-element.7) | copy-start | bytes 294916
  96.6 0.8 copy-start.1

commit v4 on v3

--- a/solution.py
+++ b/solution.py
@@ -148,11 +148,6 @@
     nt = (((1,), (1,)), ((), ()))
     partial_gram = lax.dot_general(fac, fac, nt, preferred_element_type=F32)
     fg[chan] = jnp.concatenate([partial_gram[0:32], partial_gram[32:64]], axis=1)
-    pl.semaphore_wait(barrier, len(greet))
-    for d in range(1, 8):
-        peer = lax.rem(chan + d, 8)
-        send(fg.at[chan], fg.at[chan], fg_s, fg_r, (cuts, peer))
-
     zero_fac = jnp.zeros_like(fac)
     fac2 = jnp.concatenate(
         [jnp.concatenate([fac, zero_fac], axis=1), jnp.concatenate([zero_fac, fac], axis=1)], axis=0
@@ -164,6 +159,11 @@
         out = lax.dot_general(jnp.concatenate([first, second], axis=1), fac2, nt, preferred_element_type=F32)
         for c in range(8):
             psend[j, c % 4, c // 4] = out[48 * c : 48 * c + 48]
+    pl.semaphore_wait(barrier, len(greet))
+    for d in range(1, 8):
+        peer = lax.rem(chan + d, 8)
+        send(fg.at[chan], fg.at[chan], fg_s, fg_r, (cuts, peer))
+    for j in range(4):
         for d in (2, 1, 3):
             to = lax.rem(xx + d, 4)
             send(psend.at[j, to], precv.at[j, xx], px_s, px_r.at[j], (cuts, yhi * 4 + to))
@@ -210,9 +210,11 @@
         x_s[j] = CHEB_A * eye + CHEB_B * system
 
     def newton(step, carry):
-        for j in range(4):
-            x = x_s[j]
-            x_s[j] = mm(x, 2.0 * eye - dot(sys_s[j], rhs3(x)))
+        xs = [x_s[j] for j in range(4)]
+        gaps = [2.0 * eye - dot(sys_s[j], rhs3(xs[j])) for j in range(4)]
+        fresh = [mm(xs[j], gaps[j]) for j in range(4)]
+        for j in range(4):
+            x_s[j] = fresh[j]
         return carry
 
     def forward(j):
@@ -323,13 +325,14 @@
             cr[j] = dot(lhs3(bracket), jnp.concatenate([firsts, firsts, rests], axis=0))
         return carry
 
+    fresh = []
     for j in range(4):
         arrived(yrecv.at[j], py_s, py_r.at[j])
         baux[j] = (baux[j] + yrecv[j]) * w_over[j : j + 1]
-        dual = talls[j]
-        evo = dot(lhs3(baux[j] + (aux_p[0, j] - dss[j]) + us[j]), x_rhs[j])
-        tall = evo + dual
-        evos[j] = evo
+        fresh.append(dot(lhs3(baux[j] + (aux_p[0, j] - dss[j]) + us[j]), x_rhs[j]))
+    for j in range(4):
+        tall = fresh[j] + talls[j]
+        evos[j] = fresh[j]
         talls[j] = tall
         part = narrow(gram_of([tall], [tall]))
         gsend[2 * j] = part[0:32]
@@ -349,17 +352,19 @@
         delta_t = transposed(delta)
         delta_l = lhs3(delta)
         delta_r = rhs3(delta_t)
-        scales = []
-        for j in range(4):
-            lefts = dot(delta_l, rhs3(grams[j]))
-            left_s[j] = lefts
-            normal = dot(lhs3(lefts), delta_r)
-            trace = half_sums(jnp.sum(jnp.where(eye_b, normal, 0.0), axis=0, keepdims=True)) + EPS_TRACE
+        lefts = [dot(delta_l, rhs3(grams[j])) for j in range(4)]
+        normals = [dot(lhs3(lefts[j]), delta_r) for j in range(4)]
+        scales, curs, brackets = [], [], []
+        for j in range(4):
+            left_s[j] = lefts[j]
+            trace = half_sums(jnp.sum(jnp.where(eye_b, normals[j], 0.0), axis=0, keepdims=True)) + EPS_TRACE
             scales.append(1.0 / jnp.sqrt(trace))
-            cur = normal / trace
-            bracket = 1.5 * eye - 0.5 * cur
-            cr[j, :, 0:128] = mm(bracket, cur)
-            cr[j, :, 128:256] = bracket
+            curs.append(normals[j] * (1.0 / trace))
+            brackets.append(1.5 * eye - 0.5 * curs[j])
+        firsts = [mm(brackets[j], curs[j]) for j in range(4)]
+        for j in range(4):
+            cr[j, :, 0:128] = firsts[j]
+            cr[j, :, 128:256] = brackets[j]
 
         if it == 0:
             lax.fori_loop(0, 3, polar, 0)
@@ -371,13 +376,13 @@
             lax.fori_loop(0, POLAR - 4, polar, 0)
         else:
             lax.fori_loop(0, POLAR - 2, polar, 0)
-        part = jnp.zeros((64, 128), F32)
-        for j in range(4):
-            both = cr[j]
-            root = both[:, 128:256]
-            root = mm(1.5 * eye - 0.5 * mm(root, both[:, 0:128]), root)
-            cr[j, :, 128:256] = root
-            part = part + mm(root, left_s[j]) * scales[j]
+        boths = [cr[j] for j in range(4)]
+        prods = [mm(boths[j][:, 128:256], boths[j][:, 0:128]) for j in range(4)]
+        roots = [mm(1.5 * eye - 0.5 * prods[j], boths[j][:, 128:256]) for j in range(4)]
+        parts = [mm(roots[j], left_s[j]) * scales[j] for j in range(4)]
+        for j in range(4):
+            k_s[j] = roots[j]
+        part = (parts[0] + parts[1]) + (parts[2] + parts[3])
         part = part + swap(part)
         packed = jnp.where(low, part[0:32], part[32:64])
         for q in range(4):
@@ -390,7 +395,7 @@
             gather_sums(1)
         delta_tl = lhs3(delta_t)
         for j in range(4):
-            k_s[j] = dot(delta_tl, rhs3(cr[j, :, 128:256])) * scales[j]
+            k_s[j] = dot(delta_tl, rhs3(k_s[j])) * scales[j]
         arrived(qrecv.at[it, pl.ds(0, 3)], q1_s, q1_r.at[it])
         zbuf[it * 8 + zz] = (qrecv[it, 0] + qrecv[it, 1]) + (qrecv[it, 2] + qrecv[it, 3])
         for d in (4, 3, 5, 2, 6, 1, 7):
@@ -417,32 +422,33 @@
         fresh_r = rhs3(delta)
 
         if last:
+            mixers = [dot(lhs3(k_s[j]), fresh_r) for j in range(4)]
+            coups = [mm(talls[j], mixers[j]) for j in range(4)]
             for j in range(4):
-                mixer = dot(lhs3(k_s[j]), fresh_r)
-                coup = mm(talls[j], mixer)
-                coup_o[j] = coup[:, 0:64]
-                coup_o[j + 4] = coup[:, 64:128]
+                coup_o[j] = coups[j][:, 0:64]
+                coup_o[j + 4] = coups[j][:, 64:128]
             delta_o[...] = delta[:, 0:64]
         else:
-            fresh = []
+            mixers = [dot(lhs3(k_s[j]), fresh_r) for j in range(4)]
+            turns = [dot(lhs3(2.0 * mixers[j] - eye), x_rhs[j]) for j in range(4)]
             for j in range(4):
-                mixer = dot(lhs3(k_s[j]), fresh_r)
-                turn = dot(lhs3(2.0 * mixer - eye), x_rhs[j])
-                mix_s[j, :, 0:128] = rhs3(turn)
-                mix_s[j, :, 128:256] = rhs3(mixer)
-                if it == 0:
-                    evo, tall = rows_of(j)
-                    evos[j] = evo
-                    talls[j] = tall
-                    at_s[1, j] = (evo + dss[j]) * a_rows[j : j + 1]
-                step = turn + (eye - mixer)
+                mix_s[j, :, 0:128] = rhs3(turns[j])
+                mix_s[j, :, 128:256] = rhs3(mixers[j])
+            steps = [turns[j] + (eye - mixers[j]) for j in range(4)]
+            sides = [mm(grams[j], steps[j]) for j in range(4)]
+            if it == 0:
+                fresh = [rows_of(j) for j in range(4)]
+                for j in range(4):
+                    evos[j], talls[j] = fresh[j]
+                    at_s[1, j] = (fresh[j][0] + dss[j]) * a_rows[j : j + 1]
+            grams = []
+            for j in range(4):
                 guu = jnp.concatenate([sall[it, 2 * j, 0], sall[it, 2 * j + 1, 0]], axis=0)
                 gtu = jnp.concatenate([sall[it, 2 * j, 1], sall[it, 2 * j + 1, 1]], axis=0)
-                side = gtu + 0.5 * mm(grams[j], step)
-                fresh.append(guu + narrow(gram_of([step, side], [side, step])))
+                side = gtu + 0.5 * sides[j]
+                grams.append(guu + narrow(gram_of([steps[j], side], [side, steps[j]])))
             if it == 0:
                 halo_send(at_s.at[1], hal_t.at[1], ht_s, ht_r.at[1])
-            grams = fresh
 
     for ref, ssem, rsem in (
         (psend.at[pl.ds(0, 3)], px_s, px_r.at[0]),

time: 98.2 us -> 91.1 us (0.928)
  Pallas kernels: 94.3 us -> 87.2 us
    pallas_call x1, Pallas kernels: 94.3 us -> 87.2 us  [body(): pl.pallas_call(kernel, out_shape=(jax.ShapeDtypeStruct((8, 48, 64), F32),...]
where the time goes in v4:
time: 91.1 us; the launch traced here: 90.9 us
  Pallas kernels  87.2 us (96%)
  local copies, waits for them, and re-layouts  3.03 us (3%)
    pallas_call x1, Pallas kernels, body(): pl.pallas_call(kernel, out_shape=(jax.ShapeDtypeStruct((8, 48, 64), F32),...  87.2 us
    unnamed x7, local copies, waits for them, and re-layouts  3.03 us

profile of v4, /device:TPU:1, one launch (start us, length us, event | category | flops | bytes accessed | tf_op | source)
XLA Modules:
  0.0 90.9 jit_solution(14571630760737008367)
XLA Ops:
  0.6 87.2 %shard_map.112 = (f32[8,48,64]{2,1,0:T(8,128)}, f32[8,48,64]{2,1,0:T(8,128)}, f32[64,64]{1,0:T(8,128)}) custom-call(s32[8]{0:T(128)} %order.1, bf16[8,384,128]{2,1,0:T(8,128)(2,1)} %data_h.1, bf16[64,128]{1,0:T(8,128)(2,1)} %bitcast.1, f32[8,64]{1,0:T(8,128)} %w_h.1, f32[8,48,64]{2,1,0:T(8,128)} %aux_h.1, f32[8,48,64]{2,1,0:T(8,128)} %coup_h.1, ...), custom_call_target="tpu_custom_call" | custom-call | tf_op jit(solution)/shard_map/pallas_call | solution.py:477
  87.8 0.0 copy-start
  87.8 1.7 %copy.15 = f32[8,48,64]{2,1,0:T(8,128)} copy(f32[8,48,64]{2,1,0:T(8,128)} %get-tuple-element.6) | data formatting | bytes 196608
  89.5 0.0 copy-done
  89.5 0.0 copy-start.1
  89.5 0.7 copy.16
  90.2 0.1 copy-done.1
  90.2 0.6 copy.17
Async XLA Ops:
  87.8 1.7 %copy-start = (f32[8,48,64]{2,1,0:T(8,128)S(1)}, f32[8,48,64]{2,1,0:T(8,128)}, u32[]{:S(2)}) copy-start(f32[8,48,64]{2,1,0:T(8,128)} %get-tuple-element.7) | copy-start | bytes 294916
  89.5 0.8 copy-start.1

commit v5 on v4

--- a/solution.py
+++ b/solution.py
@@ -49,7 +49,7 @@
     order, data_h, fac_h, w_h, aux_h, coup_h, ds_h, dc_h, delta_h,
     evo_o, coup_o, delta_o,
     data_v, fac_v, w_v, rows_v, delta_v,
-    psend, precv, ysend, yrecv, fg, x_s, sys_s, x_rhs, cr, left_s, k_s,
+    psend, precv, ysend, yrecv, fg, x_s, sys_s, x_rhs, cr, left_s, k_l, gram_l, gtu_s,
     gsend, grecv, gall, ssend, srecv, sall, qsend, qrecv, zbuf, qall,
     aux_p, dss, talls, evos, us, mix_s, at_s, baux, hal_a, hal_t, bsend, hal_b,
     load_sem, px_s, px_r, py_s, py_r, fg_s, fg_r, g1_s, g1_r, g2_s, g2_r, s1_s, s1_r, s2_s, s2_r,
@@ -294,11 +294,11 @@
             halo_send(aux_p.at[1], hal_a.at[1], ha_s, ha_r.at[1])
         for j in range(4):
             u, tall = us[j], talls[j]
-            guu = narrow(gram_of([u], [u]))
-            gtu = narrow(gram_of([tall], [u]))
+            sums = gram_of([u], [jnp.concatenate([u, tall], axis=1)])
+            guu, gut = narrow(sums[:, 0:128]), narrow(sums[:, 128:256])
             for h in range(2):
                 ssend[it, 2 * j + h, 0] = guu[32 * h : 32 * h + 32]
-                ssend[it, 2 * j + h, 1] = gtu[32 * h : 32 * h + 32]
+                ssend[it, 2 * j + h, 1] = gut[32 * h : 32 * h + 32]
         scatter(ssend.at[it], srecv.at[it], s1_s, s1_r.at[it])
 
     def gather_sums(it):
@@ -347,19 +347,19 @@
     from_chan(gall, g2_s, g2_r)
     grams = [jnp.concatenate([gall[2 * j], gall[2 * j + 1]], axis=0) for j in range(4)]
 
+    delta_t = transposed(delta)
     for it in range(INNER):
         last = it == INNER - 1
-        delta_t = transposed(delta)
         delta_l = lhs3(delta)
         delta_r = rhs3(delta_t)
         lefts = [dot(delta_l, rhs3(grams[j])) for j in range(4)]
+        traces = [half_sums(jnp.sum(lefts[j] * delta, axis=0, keepdims=True)) + EPS_TRACE for j in range(4)]
+        scales = [1.0 / jnp.sqrt(traces[j]) for j in range(4)]
         normals = [dot(lhs3(lefts[j]), delta_r) for j in range(4)]
-        scales, curs, brackets = [], [], []
+        curs, brackets = [], []
         for j in range(4):
             left_s[j] = lefts[j]
-            trace = half_sums(jnp.sum(jnp.where(eye_b, normals[j], 0.0), axis=0, keepdims=True)) + EPS_TRACE
-            scales.append(1.0 / jnp.sqrt(trace))
-            curs.append(normals[j] * (1.0 / trace))
+            curs.append(normals[j] * (1.0 / traces[j]))
             brackets.append(1.5 * eye - 0.5 * curs[j])
         firsts = [mm(brackets[j], curs[j]) for j in range(4)]
         for j in range(4):
@@ -371,9 +371,7 @@
             gather_sums(0)
             lax.fori_loop(0, POLAR - 5, polar, 0)
         elif it == 1:
-            lax.fori_loop(0, 2, polar, 0)
-            smooth(1)
-            lax.fori_loop(0, POLAR - 4, polar, 0)
+            lax.fori_loop(0, POLAR - 2, polar, 0)
         else:
             lax.fori_loop(0, POLAR - 2, polar, 0)
         boths = [cr[j] for j in range(4)]
@@ -381,7 +379,7 @@
         roots = [mm(1.5 * eye - 0.5 * prods[j], boths[j][:, 128:256]) for j in range(4)]
         parts = [mm(roots[j], left_s[j]) * scales[j] for j in range(4)]
         for j in range(4):
-            k_s[j] = roots[j]
+            x_s[j] = roots[j]
         part = (parts[0] + parts[1]) + (parts[2] + parts[3])
         part = part + swap(part)
         packed = jnp.where(low, part[0:32], part[32:64])
@@ -392,10 +390,13 @@
             send(qsend.at[it * 4 + to], qrecv.at[it, quad], q1_s, q1_r.at[it], quad_dev(to))
         qrecv[it, quad] = qsend[it * 4 + quad]
         if it == 1:
-            gather_sums(1)
+            smooth(1)
         delta_tl = lhs3(delta_t)
         for j in range(4):
-            k_s[j] = dot(delta_tl, rhs3(k_s[j])) * scales[j]
+            root = x_s[j]
+            k_l[j] = lhs3(dot(delta_tl, rhs3(root)) * scales[j])
+            if not last:
+                gram_l[j] = lhs3(grams[j])
         arrived(qrecv.at[it, pl.ds(0, 3)], q1_s, q1_r.at[it])
         zbuf[it * 8 + zz] = (qrecv[it, 0] + qrecv[it, 1]) + (qrecv[it, 2] + qrecv[it, 3])
         for d in (4, 3, 5, 2, 6, 1, 7):
@@ -407,6 +408,8 @@
                 talls[j] = tall
                 evo_o[j] = evo[:, 0:64]
                 evo_o[j + 4] = evo[:, 64:128]
+        if it == 1:
+            gather_sums(1)
         arrived(zbuf.at[pl.ds(it * 8, 7)], z_s, z_r.at[it])
         total = zbuf[it * 8]
         for z in range(1, 8):
@@ -417,25 +420,29 @@
             send(slot, slot, q2_s, q2_r.at[it], quad_dev(lax.rem(quad + d, 4)))
         if not last:
             from_chan(sall.at[it], s2_s, s2_r.at[it])
+            for j in range(4):
+                gut = jnp.concatenate([sall[it, 2 * j, 1], sall[it, 2 * j + 1, 1]], axis=0)
+                gtu_s[j] = narrow(jnp.concatenate([gut, gut], axis=0).T)
         arrived(qall.at[pl.ds(it * 4, 3)], q2_s, q2_r.at[it])
         delta = unpack(jnp.concatenate([qall[it * 4 + q] for q in range(4)], axis=0))
         fresh_r = rhs3(delta)
 
         if last:
-            mixers = [dot(lhs3(k_s[j]), fresh_r) for j in range(4)]
+            mixers = [dot(k_l[j], fresh_r) for j in range(4)]
             coups = [mm(talls[j], mixers[j]) for j in range(4)]
             for j in range(4):
                 coup_o[j] = coups[j][:, 0:64]
                 coup_o[j + 4] = coups[j][:, 64:128]
             delta_o[...] = delta[:, 0:64]
         else:
-            mixers = [dot(lhs3(k_s[j]), fresh_r) for j in range(4)]
+            mixers = [dot(k_l[j], fresh_r) for j in range(4)]
             turns = [dot(lhs3(2.0 * mixers[j] - eye), x_rhs[j]) for j in range(4)]
             for j in range(4):
                 mix_s[j, :, 0:128] = rhs3(turns[j])
                 mix_s[j, :, 128:256] = rhs3(mixers[j])
             steps = [turns[j] + (eye - mixers[j]) for j in range(4)]
-            sides = [mm(grams[j], steps[j]) for j in range(4)]
+            sides = [gtu_s[j] + 0.5 * dot(gram_l[j], rhs3(steps[j])) for j in range(4)]
+            delta_t = transposed(delta)
             if it == 0:
                 fresh = [rows_of(j) for j in range(4)]
                 for j in range(4):
@@ -444,9 +451,7 @@
             grams = []
             for j in range(4):
                 guu = jnp.concatenate([sall[it, 2 * j, 0], sall[it, 2 * j + 1, 0]], axis=0)
-                gtu = jnp.concatenate([sall[it, 2 * j, 1], sall[it, 2 * j + 1, 1]], axis=0)
-                side = gtu + 0.5 * sides[j]
-                grams.append(guu + narrow(gram_of([steps[j], side], [side, steps[j]])))
+                grams.append(guu + narrow(gram_of([steps[j], sides[j]], [sides[j], steps[j]])))
             if it == 0:
                 halo_send(at_s.at[1], hal_t.at[1], ht_s, ht_r.at[1])
 
@@ -487,7 +492,8 @@
             vm((8, 384, 128), BF16), vm((64, 128), BF16), vm((8, 64), F32), vm((4, 8, 48, 64), F32), vm((64, 64), F32),
             vm((4, 4, 2, 48, 128), F32), vm((4, 4, 2, 48, 128), F32), vm(rows, F32), vm(rows, F32),
             vm((8, 32, 128), F32), vm((4, 64, 128), F32), vm((4, 64, 384), BF16), vm((4, 384, 128), BF16),
-            vm((4, 64, 256), F32), vm((4, 64, 128), F32), vm((4, 64, 128), F32),
+            vm((4, 64, 256), F32), vm((4, 64, 128), F32), vm((4, 64, 384), BF16),
+            vm((4, 64, 384), BF16), vm((4, 64, 128), F32),
             vm((8, 32, 128), F32), vm((8, 32, 128), F32), vm((8, 32, 128), F32),
             vm((2, 8, 2, 32, 128), F32), vm((2, 8, 2, 32, 128), F32), vm((2, 8, 2, 32, 128), F32),
             vm((12, 8, 128), F32), vm((3, 4, 8, 128), F32), vm((24, 8, 128), F32), vm((12, 8, 128), F32),

time: 91.1 us -> 91.2 us (level)
  no operation moved by 1% of the time
where the time goes in v5:
time: 91.2 us; the launch traced here: 91 us
  Pallas kernels  87.3 us (96%)
  local copies, waits for them, and re-layouts  3.03 us (3%)
    pallas_call x1, Pallas kernels, body(): pl.pallas_call(kernel, out_shape=(jax.ShapeDtypeStruct((8, 48, 64), F32),...  87.3 us
    unnamed x7, local copies, waits for them, and re-layouts  3.03 us

profile of v5, /device:TPU:1, one launch (start us, length us, event | category | flops | bytes accessed | tf_op | source)
XLA Modules:
  0.0 91.0 jit_solution(4605476252155778182)
XLA Ops:
  0.6 87.3 %shard_map.112 = (f32[8,48,64]{2,1,0:T(8,128)}, f32[8,48,64]{2,1,0:T(8,128)}, f32[64,64]{1,0:T(8,128)}) custom-call(s32[8]{0:T(128)} %order.1, bf16[8,384,128]{2,1,0:T(8,128)(2,1)} %data_h.1, bf16[64,128]{1,0:T(8,128)(2,1)} %bitcast.1, f32[8,64]{1,0:T(8,128)} %w_h.1, f32[8,48,64]{2,1,0:T(8,128)} %aux_h.1, f32[8,48,64]{2,1,0:T(8,128)} %coup_h.1, ...), custom_call_target="tpu_custom_call" | custom-call | tf_op jit(solution)/shard_map/pallas_call | solution.py:482
  88.0 0.0 copy-start
  88.0 1.7 %copy.15 = f32[8,48,64]{2,1,0:T(8,128)} copy(f32[8,48,64]{2,1,0:T(8,128)} %get-tuple-element.6) | data formatting | bytes 196608
  89.6 0.0 copy-done
  89.6 0.0 copy-start.1
  89.6 0.7 copy.16
  90.3 0.1 copy-done.1
  90.4 0.6 copy.17
Async XLA Ops:
  88.0 1.7 %copy-start = (f32[8,48,64]{2,1,0:T(8,128)S(1)}, f32[8,48,64]{2,1,0:T(8,128)}, u32[]{:S(2)}) copy-start(f32[8,48,64]{2,1,0:T(8,128)} %get-tuple-element.7) | copy-start | bytes 294916
  89.6 0.8 copy-start.1

commit v6 on v5

--- a/solution.py
+++ b/solution.py
@@ -47,7 +47,7 @@
 
 def kernel(
     order, data_h, fac_h, w_h, aux_h, coup_h, ds_h, dc_h, delta_h,
-    evo_o, coup_o, delta_o,
+    out_o, delta_o,
     data_v, fac_v, w_v, rows_v, delta_v,
     psend, precv, ysend, yrecv, fg, x_s, sys_s, x_rhs, cr, left_s, k_l, gram_l, gtu_s,
     gsend, grecv, gall, ssend, srecv, sall, qsend, qrecv, zbuf, qall,
@@ -344,10 +344,10 @@
     from_chan(grecv, g1_s, g1_r)
     spread(gall, g2_s, g2_r, total_of(grecv))
     smooth(0)
+    delta_t = transposed(delta)
     from_chan(gall, g2_s, g2_r)
     grams = [jnp.concatenate([gall[2 * j], gall[2 * j + 1]], axis=0) for j in range(4)]
 
-    delta_t = transposed(delta)
     for it in range(INNER):
         last = it == INNER - 1
         delta_l = lhs3(delta)
@@ -371,7 +371,9 @@
             gather_sums(0)
             lax.fori_loop(0, POLAR - 5, polar, 0)
         elif it == 1:
-            lax.fori_loop(0, POLAR - 2, polar, 0)
+            lax.fori_loop(0, 2, polar, 0)
+            smooth(1)
+            lax.fori_loop(0, POLAR - 4, polar, 0)
         else:
             lax.fori_loop(0, POLAR - 2, polar, 0)
         boths = [cr[j] for j in range(4)]
@@ -390,7 +392,7 @@
             send(qsend.at[it * 4 + to], qrecv.at[it, quad], q1_s, q1_r.at[it], quad_dev(to))
         qrecv[it, quad] = qsend[it * 4 + quad]
         if it == 1:
-            smooth(1)
+            gather_sums(1)
         delta_tl = lhs3(delta_t)
         for j in range(4):
             root = x_s[j]
@@ -406,10 +408,7 @@
             for j in range(4):
                 evo, tall = rows_of(j)
                 talls[j] = tall
-                evo_o[j] = evo[:, 0:64]
-                evo_o[j + 4] = evo[:, 64:128]
-        if it == 1:
-            gather_sums(1)
+                out_o[j] = evo
         arrived(zbuf.at[pl.ds(it * 8, 7)], z_s, z_r.at[it])
         total = zbuf[it * 8]
         for z in range(1, 8):
@@ -431,8 +430,7 @@
             mixers = [dot(k_l[j], fresh_r) for j in range(4)]
             coups = [mm(talls[j], mixers[j]) for j in range(4)]
             for j in range(4):
-                coup_o[j] = coups[j][:, 0:64]
-                coup_o[j + 4] = coups[j][:, 64:128]
+                out_o[4 + j] = coups[j]
             delta_o[...] = delta[:, 0:64]
         else:
             mixers = [dot(k_l[j], fresh_r) for j in range(4)]
@@ -473,21 +471,27 @@
         whole(ref, ssem, rsem).wait_send()
 
 
+def unpair(out_p, delta_p, evo_o, coup_o, delta_o):
+    for j in range(4):
+        evo, coup = out_p[j], out_p[4 + j]
+        evo_o[j] = evo[:, 0:64]
+        evo_o[j + 4] = evo[:, 64:128]
+        coup_o[j] = coup[:, 0:64]
+        coup_o[j + 4] = coup[:, 64:128]
+    delta_o[...] = delta_p[...]
+
+
 def body(data, order, chan_factor, slice_weights, smooth_aux, coupled, smooth_dual, coupling_dual, delta):
     vm = pltpu.VMEM
     dma = pltpu.SemaphoreType.DMA
     rows = (4, 48, 128)
     anyspace = pl.BlockSpec(memory_space=pl.ANY)
     vspace = pl.BlockSpec(memory_space=pltpu.VMEM)
-    return pl.pallas_call(
+    paired, delta_out = pl.pallas_call(
         kernel,
-        out_shape=(
-            jax.ShapeDtypeStruct((8, 48, 64), F32),
-            jax.ShapeDtypeStruct((8, 48, 64), F32),
-            jax.ShapeDtypeStruct((64, 64), F32),
-        ),
+        out_shape=(jax.ShapeDtypeStruct((8, 48, 128), F32), jax.ShapeDtypeStruct((64, 64), F32)),
         in_specs=[pl.BlockSpec(memory_space=pltpu.SMEM)] + [anyspace] * 8,
-        out_specs=(vspace, vspace, vspace),
+        out_specs=(vspace, vspace),
         scratch_shapes=[
             vm((8, 384, 128), BF16), vm((64, 128), BF16), vm((8, 64), F32), vm((4, 8, 48, 64), F32), vm((64, 64), F32),
             vm((4, 4, 2, 48, 128), F32), vm((4, 4, 2, 48, 128), F32), vm(rows, F32), vm(rows, F32),
@@ -507,6 +511,16 @@
             collective_id=0, has_side_effects=True, vmem_limit_bytes=60 * 1024 * 1024
         ),
     )(order, data, chan_factor.T, slice_weights, smooth_aux, coupled, smooth_dual, coupling_dual, delta)
+    return pl.pallas_call(
+        unpair,
+        out_shape=(
+            jax.ShapeDtypeStruct((8, 48, 64), F32),
+            jax.ShapeDtypeStruct((8, 48, 64), F32),
+            jax.ShapeDtypeStruct((64, 64), F32),
+        ),
+        in_specs=[vspace, vspace],
+        out_specs=(vspace, vspace, vspace),
+    )(paired, delta_out)
 
 
 def solution(mesh):

time: 91.2 us -> 89.4 us (0.980)
  local copies, waits for them, and re-layouts: 3.03 us -> 0 us
  Pallas kernels: 87.3 us -> 88.6 us
    unnamed x7 -> x0, local copies, waits for them, and re-layouts: 3.03 us -> none
    pallas_call x1 -> x2, Pallas kernels: 87.3 us -> 88.6 us  [the longest x1 86.8 us: body(): pl.pallas_call(kernel, out_shape=(jax.ShapeDtypeStruct((8, 48, 128), F32)...]
where the time goes in v6:
time: 89.4 us; the launch traced here: 89.2 us
  Pallas kernels  88.6 us (99%)
    pallas_call x1, Pallas kernels, body(): pl.pallas_call(kernel, out_shape=(jax.ShapeDtypeStruct((8, 48, 128), F32)...  86.8 us

profile of v6, /device:TPU:1, one launch (start us, length us, event | category | flops | bytes accessed | tf_op | source)
XLA Modules:
  0.0 89.2 jit_solution(14205677240112673028)
XLA Ops:
  0.6 86.8 %shard_map.112 = (f32[8,48,128]{2,1,0:T(8,128)}, f32[64,64]{1,0:T(8,128)}) custom-call(s32[8]{0:T(128)} %order.1, bf16[8,384,128]{2,1,0:T(8,128)(2,1)} %data_h.1, bf16[64,128]{1,0:T(8,128)(2,1)} %bitcast.1, f32[8,64]{1,0:T(8,128)} %w_h.1, f32[8,48,64]{2,1,0:T(8,128)} %aux_h.1, f32[8,48,64]{2,1,0:T(8,128)} %coup_h.1, f32[8,48,64]{2,1,0:T(8,128)} %ds_h.1, ...), custom_call_target="tpu_custom_call" | custom-call | tf_op jit(solution)/shard_map/pallas_call | solution.py:490
  87.4 1.8 %shard_map.113 = (f32[8,48,64]{2,1,0:T(8,128)}, f32[8,48,64]{2,1,0:T(8,128)}, f32[64,64]{1,0:T(8,128)}) custom-call(f32[8,48,128]{2,1,0:T(8,128)} %get-tuple-element.5.out_p, f32[64,64]{1,0:T(8,128)} %get-tuple-element.6.delta_p), custom_call_target="tpu_custom_call" | custom-call | tf_op jit(solution)/shard_map/pallas_call | solution.py:514

commit v7 on v6

--- a/solution.py
+++ b/solution.py
@@ -50,10 +50,10 @@
     out_o, delta_o,
     data_v, fac_v, w_v, rows_v, delta_v,
     psend, precv, ysend, yrecv, fg, x_s, sys_s, x_rhs, cr, left_s, k_l, gram_l, gtu_s,
-    gsend, grecv, gall, ssend, srecv, sall, qsend, qrecv, zbuf, qall,
+    gsend, grecv, gall, ssend, srecv, sall, qsend, qrecv, zbuf,
     aux_p, dss, talls, evos, us, mix_s, at_s, baux, hal_a, hal_t, bsend, hal_b,
     load_sem, px_s, px_r, py_s, py_r, fg_s, fg_r, g1_s, g1_r, g2_s, g2_r, s1_s, s1_r, s2_s, s2_r,
-    q1_s, q1_r, z_s, z_r, q2_s, q2_r, ha_s, ha_r, ht_s, ht_r, hb_s, hb_r,
+    q1_s, q1_r, z_s, z_r, ha_s, ha_r, ht_s, ht_r, hb_s, hb_r,
 ):
     cuts = lax.axis_index("cuts")
     chan = lax.axis_index("chan")
@@ -97,9 +97,7 @@
 
     barrier = pltpu.get_barrier_semaphore()
     greet = [(cuts, lax.rem(chan + d, 8)) for d in range(1, 8)]
-    greet += [z_dev(lax.rem(zz + d, 8)) for d in range(1, 8)]
-    greet += [quad_dev(lax.rem(quad + d, 4)) for d in range(1, 4)]
-    greet += [(left_id, chan), (right_id, chan)]
+    greet += [(lax.rem(cuts + d, 32), chan) for d in range(1, 32)]
     for dev in greet:
         pl.semaphore_signal(barrier, inc=1, device_id=dev, device_id_type=MESH)
 
@@ -400,30 +398,33 @@
             if not last:
                 gram_l[j] = lhs3(grams[j])
         arrived(qrecv.at[it, pl.ds(0, 3)], q1_s, q1_r.at[it])
-        zbuf[it * 8 + zz] = (qrecv[it, 0] + qrecv[it, 1]) + (qrecv[it, 2] + qrecv[it, 3])
-        for d in (4, 3, 5, 2, 6, 1, 7):
-            slot = zbuf.at[it * 8 + zz]
-            send(slot, slot, z_s, z_r.at[it], z_dev(lax.rem(zz + d, 8)))
+        mine = zbuf.at[it * 32 + zz * 4 + quad]
+        mine[...] = (qrecv[it, 0] + qrecv[it, 1]) + (qrecv[it, 2] + qrecv[it, 3])
+        for d in (4, 3, 5, 2, 6, 1, 7, 0):
+            z = lax.rem(zz + d, 8)
+            for e in range(4):
+                if d + e:
+                    q = lax.rem(quad + e, 4)
+                    dev = ((q // 2) * 16 + z * 2 + lax.rem(q, 2), chan)
+                    send(mine, mine, z_s, z_r.at[it], dev)
         if last:
             for j in range(4):
                 evo, tall = rows_of(j)
                 talls[j] = tall
                 out_o[j] = evo
-        arrived(zbuf.at[pl.ds(it * 8, 7)], z_s, z_r.at[it])
-        total = zbuf[it * 8]
-        for z in range(1, 8):
-            total = total + zbuf[it * 8 + z]
-        qall[it * 4 + quad] = total * (1.0 / 256.0)
-        for d in range(1, 4):
-            slot = qall.at[it * 4 + quad]
-            send(slot, slot, q2_s, q2_r.at[it], quad_dev(lax.rem(quad + d, 4)))
         if not last:
             from_chan(sall.at[it], s2_s, s2_r.at[it])
             for j in range(4):
                 gut = jnp.concatenate([sall[it, 2 * j, 1], sall[it, 2 * j + 1, 1]], axis=0)
                 gtu_s[j] = narrow(jnp.concatenate([gut, gut], axis=0).T)
-        arrived(qall.at[pl.ds(it * 4, 3)], q2_s, q2_r.at[it])
-        delta = unpack(jnp.concatenate([qall[it * 4 + q] for q in range(4)], axis=0))
+        arrived(zbuf.at[pl.ds(it * 32, 31)], z_s, z_r.at[it])
+        packed = []
+        for q in range(4):
+            total = zbuf[it * 32 + q]
+            for z in range(1, 8):
+                total = total + zbuf[it * 32 + 4 * z + q]
+            packed.append(total * (1.0 / 256.0))
+        delta = unpack(jnp.concatenate(packed, axis=0))
         fresh_r = rhs3(delta)
 
         if last:
@@ -462,8 +463,7 @@
         (ssend.at[:, pl.ds(0, 7)], s1_s, s1_r.at[0]),
         (sall.at[:, pl.ds(0, 7)], s2_s, s2_r.at[0]),
         (qsend.at[pl.ds(0, 9)], q1_s, q1_r.at[0]),
-        (zbuf.at[pl.ds(0, 21)], z_s, z_r.at[0]),
-        (qall.at[pl.ds(0, 9)], q2_s, q2_r.at[0]),
+        (zbuf.at[pl.ds(0, 93)], z_s, z_r.at[0]),
         (hal_a, ha_s, ha_r.at[0]),
         (hal_t, ht_s, ht_r.at[0]),
         (hal_b, hb_s, hb_r),
@@ -500,12 +500,12 @@
             vm((4, 64, 384), BF16), vm((4, 64, 128), F32),
             vm((8, 32, 128), F32), vm((8, 32, 128), F32), vm((8, 32, 128), F32),
             vm((2, 8, 2, 32, 128), F32), vm((2, 8, 2, 32, 128), F32), vm((2, 8, 2, 32, 128), F32),
-            vm((12, 8, 128), F32), vm((3, 4, 8, 128), F32), vm((24, 8, 128), F32), vm((12, 8, 128), F32),
+            vm((12, 8, 128), F32), vm((3, 4, 8, 128), F32), vm((96, 8, 128), F32),
             vm((2,) + rows, F32), vm(rows, F32), vm(rows, F32), vm(rows, F32), vm(rows, F32), vm((4, 384, 256), BF16),
             vm((2,) + rows, F32), vm(rows, F32),
             vm((2, 2) + rows, F32), vm((2, 2) + rows, F32), vm((8, 128), F32), vm((2, 8, 128), F32),
             dma((5,)), dma, dma((4,)), dma, dma((4,)), dma, dma, dma, dma, dma, dma, dma, dma((2,)), dma, dma((2,)),
-            dma, dma((3,)), dma, dma((3,)), dma, dma((3,)), dma, dma((2,)), dma, dma((2,)), dma, dma,
+            dma, dma((3,)), dma, dma((3,)), dma, dma((2,)), dma, dma((2,)), dma, dma,
         ],
         compiler_params=pltpu.CompilerParams(
             collective_id=0, has_side_effects=True, vmem_limit_bytes=60 * 1024 * 1024

time: 89.4 us -> 87.3 us (0.977)
  Pallas kernels: 88.6 us -> 86.5 us
    pallas_call x1, Pallas kernels: 86.8 us -> 84.8 us  [body(): pl.pallas_call(kernel, out_shape=(jax.ShapeDtypeStruct((8, 48, 128), F32)...]
where the time goes in v7:
time: 87.3 us; the launch traced here: 87.2 us
  Pallas kernels  86.5 us (99%)
    pallas_call x1, Pallas kernels, body(): pl.pallas_call(kernel, out_shape=(jax.ShapeDtypeStruct((8, 48, 128), F32)...  84.8 us
    pallas_call x1, Pallas kernels, body(): pl.pallas_call(unpair, out_shape=(jax.ShapeDtypeStruct((8, 48, 64), F32),...  1.79 us

profile of v7, /device:TPU:1, one launch (start us, length us, event | category | flops | bytes accessed | tf_op | source)
XLA Modules:
  0.0 87.2 jit_solution(6375201646051967090)
XLA Ops:
  0.6 84.8 %shard_map.112 = (f32[8,48,128]{2,1,0:T(8,128)}, f32[64,64]{1,0:T(8,128)}) custom-call(s32[8]{0:T(128)} %order.1, bf16[8,384,128]{2,1,0:T(8,128)(2,1)} %data_h.1, bf16[64,128]{1,0:T(8,128)(2,1)} %bitcast.1, f32[8,64]{1,0:T(8,128)} %w_h.1, f32[8,48,64]{2,1,0:T(8,128)} %aux_h.1, f32[8,48,64]{2,1,0:T(8,128)} %coup_h.1, f32[8,48,64]{2,1,0:T(8,128)} %ds_h.1, ...), custom_call_target="tpu_custom_call" | custom-call | tf_op jit(solution)/shard_map/pallas_call | solution.py:490
  85.4 1.8 %shard_map.113 = (f32[8,48,64]{2,1,0:T(8,128)}, f32[8,48,64]{2,1,0:T(8,128)}, f32[64,64]{1,0:T(8,128)}) custom-call(f32[8,48,128]{2,1,0:T(8,128)} %get-tuple-element.5.out_p, f32[64,64]{1,0:T(8,128)} %get-tuple-element.6.delta_p), custom_call_target="tpu_custom_call" | custom-call | tf_op jit(solution)/shard_map/pallas_call | solution.py:514

commit v8 on v7

--- a/solution.py
+++ b/solution.py
@@ -8,6 +8,7 @@
 INNER = 3
 POLAR = 8
 NEWTON = 7
+FAR_FIRST = (6, 2, 5, 3, 4, 7, 1)
 EPS_TRACE = 1e-06
 F32 = jnp.float32
 MESH = pl.DeviceIdType.MESH
@@ -158,7 +159,7 @@
         for c in range(8):
             psend[j, c % 4, c // 4] = out[48 * c : 48 * c + 48]
     pl.semaphore_wait(barrier, len(greet))
-    for d in range(1, 8):
+    for d in FAR_FIRST:
         peer = lax.rem(chan + d, 8)
         send(fg.at[chan], fg.at[chan], fg_s, fg_r, (cuts, peer))
     for j in range(4):
@@ -242,11 +243,11 @@
 
     def spread(buf, ssem, rsem, own):
         buf[chan] = own
-        for d in range(1, 8):
+        for d in FAR_FIRST:
             send(buf.at[chan], buf.at[chan], ssem, rsem, (cuts, lax.rem(chan + d, 8)))
 
     def scatter(src, dst, ssem, rsem):
-        for d in range(1, 8):
+        for d in FAR_FIRST:
             peer = lax.rem(chan + d, 8)
             send(src.at[peer], dst.at[chan], ssem, rsem, (cuts, peer))
         dst[chan] = src[chan]

time: 87.3 us -> 88.3 us (1.011)
  Pallas kernels: 86.5 us -> 87.5 us
    pallas_call x1, Pallas kernels: 84.8 us -> 85.7 us  [body(): pl.pallas_call(kernel, out_shape=(jax.ShapeDtypeStruct((8, 48, 128), F32)...]
where the time goes in v8:
time: 88.3 us; the launch traced here: 88.1 us
  Pallas kernels  87.5 us (99%)
    pallas_call x1, Pallas kernels, body(): pl.pallas_call(kernel, out_shape=(jax.ShapeDtypeStruct((8, 48, 128), F32)...  85.7 us
    pallas_call x1, Pallas kernels, body(): pl.pallas_call(unpair, out_shape=(jax.ShapeDtypeStruct((8, 48, 64), F32),...  1.79 us

profile of v8, /device:TPU:1, one launch (start us, length us, event | category | flops | bytes accessed | tf_op | source)
XLA Modules:
  0.0 88.1 jit_solution(5316592633507269068)
XLA Ops:
  0.6 85.7 %shard_map.112 = (f32[8,48,128]{2,1,0:T(8,128)}, f32[64,64]{1,0:T(8,128)}) custom-call(s32[8]{0:T(128)} %order.1, bf16[8,384,128]{2,1,0:T(8,128)(2,1)} %data_h.1, bf16[64,128]{1,0:T(8,128)(2,1)} %bitcast.1, f32[8,64]{1,0:T(8,128)} %w_h.1, f32[8,48,64]{2,1,0:T(8,128)} %aux_h.1, f32[8,48,64]{2,1,0:T(8,128)} %coup_h.1, f32[8,48,64]{2,1,0:T(8,128)} %ds_h.1, ...), custom_call_target="tpu_custom_call" | custom-call | tf_op jit(solution)/shard_map/pallas_call | solution.py:491
  86.3 1.8 %shard_map.113 = (f32[8,48,64]{2,1,0:T(8,128)}, f32[8,48,64]{2,1,0:T(8,128)}, f32[64,64]{1,0:T(8,128)}) custom-call(f32[8,48,128]{2,1,0:T(8,128)} %get-tuple-element.5.out_p, f32[64,64]{1,0:T(8,128)} %get-tuple-element.6.delta_p), custom_call_target="tpu_custom_call" | custom-call | tf_op jit(solution)/shard_map/pallas_call | solution.py:515
